TPU v7x, 768 devices: a whole 4x8x12 slice. The times are simulated.
768 devices in a mesh: wave: 12 (over z), lev: 64 (over y, x, core).
Axes of the slice: x: 4, y: 8, z: 12, core: 2. Of those that a mesh axis runs over, the one named last changes fastest.
Arguments:
- spec: bfloat16 [24, 64, 2, 1280], P('wave', 'lev'), may hold values from -0.59765625 to 0.59765625
- legendre: bfloat16 [24, 1280, 1200], P('wave', 'lev'), may hold values from -0.15625 to 0.15625
- gauss_w: float32 [1200], replicated, may hold values from 0.5 to 1.5
- cycle_len: int32 [1200], replicated, may hold values from 20 to 4816, as said below
- wave_map: int32 [24], replicated, may hold values from 0 to 23, as said below
Outputs:
- grid: bfloat16 [2, 600, 64, 4864], P(None, 'wave', 'lev')
- spec_out: float32 [24, 64, 2, 1280], P('wave', 'lev')
Inputs may be any that keep to these rules, and one draw needn't show every extreme that they name: `wave_map`: A permutation of 0 .. 23; slot r of each index of wave (slots are numbered 2 to an index) holds a value from the r-th group of 12 consecutive values. `cycle_len`: entry 2r is the point count of the r-th cycle from the pole, entry 2r + 1 that of cycle 1200 - 1 - r; cycle j has a multiple of 4 points between max(20, 8 + 4 j) and 20 + 4 j, and cycle 1200 - 1 exactly 20 + 4 (1199); the southern cycle mirrors the northern one.
All inputs are finite; a program needn't handle non-finite values.
Results may differ from a plain program's by a relative error of at most 0.0055.
Values may be sent and summed in bfloat16 or wider, within the bound.
A program may use at most 32 MiB of HBM per device.

v0:
```python
import math

import jax
import jax.numpy as jnp
from jax import lax
from jax.sharding import PartitionSpec as P

LPAD = 4864


def block_rows():
    for candidate in (10, 8, 6, 5, 4, 3, 2):
        return candidate
    return 1


def cycle_tables(lens_pair, orders, padded):
    position = jnp.arange(padded, dtype=jnp.int32)[None, :]
    first_len = lens_pair[:, 0:1]
    second = lens_pair[:, 1:2]
    upper_half = position >= first_len
    occupied = position < first_len + second
    offset = jnp.where(upper_half, position - first_len, position)
    length = jnp.where(upper_half, second, first_len)
    turn_count = orders[None, :, None] * offset[:, None, :] % length[:, None, :]
    angles = 2.0 * math.pi * turn_count.astype(jnp.float32) / length[:, None, :].astype(jnp.float32)
    cosine = jnp.where(occupied[:, None, :], jnp.cos(angles), 0.0).astype(jnp.bfloat16)
    minus_sine = jnp.where(occupied[:, None, :], -jnp.sin(angles), 0.0).astype(jnp.bfloat16)
    return (jnp.concatenate([cosine, minus_sine], 1), upper_half, occupied)


def cycle_block(waves, lens_pair, weights, orders, padded):
    row_count = waves.shape[0]
    fields = waves.shape[3]
    slot_count = orders.shape[0]
    tables, upper_half, occupied = cycle_tables(lens_pair, orders, padded)
    double = jnp.where(orders == 0, 1.0, 2.0)
    resolved = 2 * orders[None, None, :] < lens_pair[:, :, None]
    widening = jnp.where(resolved, double[None, None, :], 0.0)
    scaled = (waves.astype(jnp.float32) * widening[:, None, :, None, None, :]).astype(jnp.bfloat16)
    scaled = scaled.reshape(row_count, 4 * fields, 2 * slot_count)
    images = jnp.einsum("rak,rkp->rap", scaled, tables, preferred_element_type=jnp.float32)
    images = images.reshape(row_count, 2, 2, fields, padded)
    values = jnp.where(upper_half[:, None, None, :], images[:, :, 1], images[:, :, 0])
    values = jnp.where(occupied[:, None, None, :], values, 0.0).astype(jnp.bfloat16)
    squared = (values.astype(jnp.float32) * values.astype(jnp.float32)).astype(jnp.bfloat16)
    selector = jnp.stack([jnp.logical_not(upper_half), upper_half], 1)
    by_cycle = jnp.where(
        selector[:, None, :, None, :], squared[:, :, None, :, :], jnp.zeros((), jnp.bfloat16)
    )
    by_cycle = by_cycle.reshape(row_count, 4 * fields, padded)
    returned = jnp.einsum("rap,rkp->rak", by_cycle, tables, preferred_element_type=jnp.float32)
    returned = returned.reshape(row_count, 2, 2, fields, 2, slot_count)
    factor = jnp.where(
        resolved, weights[:, :, None] / lens_pair[:, :, None].astype(jnp.float32), 0.0
    )
    returned = (returned * factor[:, None, :, None, None, :]).astype(jnp.bfloat16)
    return (values, returned)


def parity_of(degree_ids, own_orders):
    return jnp.where((degree_ids[None, :] + own_orders[:, None]) % 2 == 0, 1.0, -1.0)


def per_device(spec, legendre, gauss_w, cycle_len, wave_map):
    slots_dev = spec.shape[0]
    fields = spec.shape[1]
    degrees_all = spec.shape[3]
    slot_count = wave_map.shape[0]
    orders = wave_map * degrees_all // slot_count
    wave_pos = lax.axis_index("wave")
    own_orders = lax.dynamic_slice_in_dim(orders, wave_pos * slots_dev, slots_dev)
    degrees = jnp.arange(degrees_all, dtype=jnp.int32)
    retained = degrees[None, :] >= own_orders[:, None]
    coefficients = jnp.where(retained[:, None, None, :], spec, jnp.zeros((), jnp.bfloat16))
    panels = lax.all_gather(legendre, "lev", axis=1, tiled=True)
    sign_flip = parity_of(degrees, own_orders)
    flipped = (coefficients.astype(jnp.float32) * sign_flip[:, None, None, :]).astype(jnp.bfloat16)
    stacked = jnp.stack([coefficients, flipped], 1)
    fourier = jnp.einsum(
        "shfcn,snq->shfcq", stacked, panels, preferred_element_type=jnp.float32
    ).astype(jnp.bfloat16)
    cycle_waves = lax.all_to_all(fourier, "wave", split_axis=4, concat_axis=0, tiled=True)
    local_lats = cycle_waves.shape[4]
    row_total = local_lats // 2
    lat_start = wave_pos * local_lats
    lens_here = lax.dynamic_slice_in_dim(cycle_len, lat_start, local_lats)
    weights_here = lax.dynamic_slice_in_dim(gauss_w, lat_start, local_lats)
    row_block = block_rows()
    blocks = row_total // row_block
    ordered = cycle_waves.reshape(slot_count, 2, fields, 2, row_total, 2).transpose(
        4, 1, 5, 2, 3, 0
    )
    ordered = ordered.reshape(blocks, row_block, 2, 2, fields, 2, slot_count)

    def run_block(operands):
        return cycle_block(operands[0], operands[1], operands[2], orders, LPAD)

    values, returned = lax.map(
        run_block,
        (
            ordered,
            lens_here.reshape(blocks, row_block, 2),
            weights_here.reshape(blocks, row_block, 2),
        ),
    )
    grid = values.reshape(row_total, 2, fields, LPAD).transpose(1, 0, 2, 3)
    returned = returned.reshape(row_total, 2, 2, fields, 2, slot_count).transpose(5, 1, 3, 4, 0, 2)
    returned = returned.reshape(slot_count, 2, fields, 2, local_lats)
    spectral = lax.all_to_all(returned, "wave", split_axis=0, concat_axis=4, tiled=True)
    both = jnp.einsum("shfcq,snq->shfcn", spectral, panels, preferred_element_type=jnp.float32)
    total = both[:, 0] + sign_flip[:, None, None, :] * both[:, 1]
    spec_out = jnp.where(retained[:, None, None, :], total, 0.0)
    return (grid, spec_out)


def solution(mesh):
    placed = (P("wave", "lev", None, None), P("wave", "lev", None), P(), P(), P())
    return jax.shard_map(
        per_device,
        mesh=mesh,
        in_specs=placed,
        out_specs=(P(None, "wave", "lev", None), P("wave", "lev", None, None)),
        check_vma=False,
    )
```

profile of v0, /device:TPU:1, one launch (start us, length us, event | category | flops | bytes accessed | tf_op | source)
XLA Modules:
  0.0 549.6 jit_solution(11972134542305313998)
XLA Ops:
  10.3 101.2 %all-gather.2.cloned.1.call-done = bf16[2,1280,1200]{2,0,1:T(2,128)(2,1)} async-done(((bf16[2,20,1200]{2,0,1:T(2,128)(2,1)}), bf16[2,1280,1200]{2,0,1:T(2,128)(2,1)}) %all-gather.2.cloned.1.call-update) | async-done | bytes 6144016 | tf_op jit(solution)/shard_map/all_gather | solution.py:76
  111.5 3.9 fusion.32
  115.4 2.6 copy.60
  118.0 1.7 reshape.528
  119.7 9.9 %all-to-all-start = ((bf16[12,2,400]{2,1,0:T(2,128)(2,1)}), bf16[12,2,400]{2,1,0:T(2,128)(2,1)S(1)}, u32[]{:S(2)}, u32[]{:S(2)}) async-start(bf16[12,2,400]{2,1,0:T(2,128)(2,1)} %reshape.528), calls=%async_computation | async-start | bytes 49152 | tf_op jit(solution)/shard_map/all_to_all | solution.py:83
  131.6 7.2 %all-to-all-done = bf16[12,2,400]{2,1,0:T(2,128)(2,1)S(1)} async-done(((bf16[12,2,400]{2,1,0:T(2,128)(2,1)}), bf16[12,2,400]{2,1,0:T(2,128)(2,1)S(1)}, u32[]{:S(2)}, u32[]{:S(2)}) %all-to-all-start) | async-done | bytes 19232 | tf_op jit(solution)/shard_map/all_to_all | solution.py:83
  139.7 2.6 copy.80
  143.1 1.5 copy.63
  144.7 380.7 %while.12 = (s32[]{:T(128)}, bf16[5,10,2,1,4864]{4,2,3,1,0:T(2,128)(2,1)}, bf16[5,10,2,2,1,2,24]{6,5,3,2,1,4,0:T(2,128)(2,1)S(1)}, s32[5,10,2]{1,2,0:T(2,128)S(1...) while((s32[]{:T(128)}, ...), condition=%wide.region_1.2_spmd, body=%wide.region_0.1_spmd.sunk | while | flops 76424608 | bytes 21034924 | solution.py:99
  145.3 64.0 %select_convert_fusion.4 = (bf16[10,24,4864]{2,1,0:T(8,128)(2,1)S(1)}, bf16[10,24,4864]{2,1,0:T(8,128)(2,1)}) fusion(f32[10,4864]{1,0:T(8,128)S(1)} %get-tuple-element.170, pred[10,4864]{1,0:T(8,128)(4,1)S(1)} %get-tuple-element.171, s32[10,4864]{1,0:T(8,128)S(1)} %get-tuple-element.172, s32[10,4864]{1,0:T(8,128)S(1)} %get-tuple-element.173, ...), kind=kLoop, calls=%fused_computation.6.clone.1 | loop fusion | flops 18677760 | bytes 5350496 | tf_op jit(solution)/shard_map/while/body/eval_jaxpr/convert_element_type | solution.py:27
  209.8 2.4 fusion.59
  212.4 1.0 fusion.62
  215.0 0.9 select_n.251
  216.0 3.1 fusion.63
  221.4 64.0 %select_convert_fusion.4 = (bf16[10,24,4864]{2,1,0:T(8,128)(2,1)S(1)}, bf16[10,24,4864]{2,1,0:T(8,128)(2,1)}) fusion(f32[10,4864]{1,0:T(8,128)S(1)} %get-tuple-element.170, pred[10,4864]{1,0:T(8,128)(4,1)S(1)} %get-tuple-element.171, s32[10,4864]{1,0:T(8,128)S(1)} %get-tuple-element.172, s32[10,4864]{1,0:T(8,128)S(1)} %get-tuple-element.173, ...), kind=kLoop, calls=%fused_computation.6.clone.1 | loop fusion | flops 18677760 | bytes 5350496 | tf_op jit(solution)/shard_map/while/body/eval_jaxpr/convert_element_type | solution.py:27
  285.9 2.4 fusion.59
  288.4 1.0 fusion.62
  292.0 3.1 fusion.63
  297.5 64.0 %select_convert_fusion.4 = (bf16[10,24,4864]{2,1,0:T(8,128)(2,1)S(1)}, bf16[10,24,4864]{2,1,0:T(8,128)(2,1)}) fusion(f32[10,4864]{1,0:T(8,128)S(1)} %get-tuple-element.170, pred[10,4864]{1,0:T(8,128)(4,1)S(1)} %get-tuple-element.171, s32[10,4864]{1,0:T(8,128)S(1)} %get-tuple-element.172, s32[10,4864]{1,0:T(8,128)S(1)} %get-tuple-element.173, ...), kind=kLoop, calls=%fused_computation.6.clone.1 | loop fusion | flops 18677760 | bytes 5350496 | tf_op jit(solution)/shard_map/while/body/eval_jaxpr/convert_element_type | solution.py:27
  362.0 2.4 fusion.59
  364.5 1.0 fusion.62
  368.1 3.1 fusion.63
  373.5 64.0 %select_convert_fusion.4 = (bf16[10,24,4864]{2,1,0:T(8,128)(2,1)S(1)}, bf16[10,24,4864]{2,1,0:T(8,128)(2,1)}) fusion(f32[10,4864]{1,0:T(8,128)S(1)} %get-tuple-element.170, pred[10,4864]{1,0:T(8,128)(4,1)S(1)} %get-tuple-element.171, s32[10,4864]{1,0:T(8,128)S(1)} %get-tuple-element.172, s32[10,4864]{1,0:T(8,128)S(1)} %get-tuple-element.173, ...), kind=kLoop, calls=%fused_computation.6.clone.1 | loop fusion | flops 18677760 | bytes 5350496 | tf_op jit(solution)/shard_map/while/body/eval_jaxpr/convert_element_type | solution.py:27
  438.1 2.4 fusion.59
  440.6 1.0 fusion.62
  444.2 3.1 fusion.63
  449.6 64.0 %select_convert_fusion.4 = (bf16[10,24,4864]{2,1,0:T(8,128)(2,1)S(1)}, bf16[10,24,4864]{2,1,0:T(8,128)(2,1)}) fusion(f32[10,4864]{1,0:T(8,128)S(1)} %get-tuple-element.170, pred[10,4864]{1,0:T(8,128)(4,1)S(1)} %get-tuple-element.171, s32[10,4864]{1,0:T(8,128)S(1)} %get-tuple-element.172, s32[10,4864]{1,0:T(8,128)S(1)} %get-tuple-element.173, ...), kind=kLoop, calls=%fused_computation.6.clone.1 | loop fusion | flops 18677760 | bytes 5350496 | tf_op jit(solution)/shard_map/while/body/eval_jaxpr/convert_element_type | solution.py:27
  514.2 2.4 fusion.59
  516.7 1.0 fusion.62
  520.3 3.1 fusion.63
  525.5 11.8 %all_to_all.30 = bf16[24,2,1,2,100]{4,3,2,1,0:T(2,128)(2,1)S(1)} all-to-all(bf16[24,2,1,2,100]{4,3,2,1,0:T(2,128)(2,1)S(1)} %copy.68), channel_id=1, replica_groups=mesh['wave'=12,'lev'=64] {'wave'}, dimensions={0} | all-to-all | bytes 38400 | tf_op jit(solution)/shard_map/all_to_all | solution.py:110
  537.4 4.7 fusion.26
  (144 shorter events, 34.4 us)
Async XLA Ops:
  7.2 104.4 %all-gather.2.cloned.1.call-start = ((), (), s32[]{:S(2)}) async-start(), calls=%async_computation.2 | async-start | bytes 6656000 | tf_op jit(solution)/shard_map/all_gather | solution.py:76
  119.7 19.2 %all-to-all-start = ((bf16[12,2,400]{2,1,0:T(2,128)(2,1)}), bf16[12,2,400]{2,1,0:T(2,128)(2,1)S(1)}, u32[]{:S(2)}, u32[]{:S(2)}) async-start(bf16[12,2,400]{2,1,0:T(2,128)(2,1)} %reshape.528), calls=%async_computation | async-start | bytes 49152 | tf_op jit(solution)/shard_map/all_to_all | solution.py:83
Sparse Core Ops, SparseCore 0:
  11.8 99.6 all-gather.1
where the time goes:
time: 551 us; the launch traced here: 550 us
  other arithmetic  342 us (62%)
  waiting for transfers between devices  109 us (20%)
  matrix products  36 us (7%)
  local copies, waits for them, and re-layouts  25.8 us (5%)
  between operations  14.2 us (3%)
  blocking collectives  11.8 us (2%)
  starting transfers between devices  9.94 us (2%)
    convert_element_type x5, other arithmetic, cycle_tables(): jnp.where(occupied[:, None, :], jnp.cos(angles), 0.0).astype(jnp.bfloat16)  320 us
    all_gather x1, waiting for transfers between devices, per_device(): panels = lax.all_gather(legendre, 'lev', axis=1, tiled=True)  101 us
    dot_general x5, matrix products, cycle_block(): jnp.einsum('rap,rkp->rak', by_cycle, tables, preferred_element_type=jnp.f...  15.5 us
    dot_general x5, matrix products, cycle_block(): jnp.einsum('rak,rkp->rap', scaled, tables, preferred_element_type=jnp.flo...  12 us
    all_to_all x1, blocking collectives, per_device(): lax.all_to_all(returned, 'wave', split_axis=0, concat_axis=4, tiled=True)  11.8 us
  transfers between devices with their start and end apart: 2, of which 2 were waited for; matrix products, arithmetic and copies ran while one was open for 1% of the time, Pallas kernels for 0%

commit v1 on v0

v1 whole, which is shorter than its diff:
```python
import math

import jax
import jax.numpy as jnp
from jax import lax
from jax.experimental import pallas as pl
from jax.experimental.pallas import tpu as pltpu
from jax.sharding import PartitionSpec as P

LPAD = 4864
LANES = 128
BLOCKS = LPAD // LANES
ROWS = 2 * BLOCKS
ROWS_PAD = 80
SLOT_PAD = 32


def parity_of(degree_ids, own_orders):
    return jnp.where((degree_ids[None, :] + own_orders[:, None]) % 2 == 0, 1.0, -1.0)


def cos_sin_turns(turns):
    quarter = turns * 4.0
    whole = jnp.round(quarter)
    rest = (quarter - whole) * (0.5 * math.pi)
    square = rest * rest
    sine = rest + rest * square * (
        -1.6666666666e-1 + square * (8.3333331e-3 + square * (-1.98412698e-4 + square * 2.7557319e-6))
    )
    cosine = 1.0 + square * (
        -0.5 + square * (4.16666667e-2 + square * (-1.388888889e-3 + square * (2.48015873e-5 - square * 2.7557319e-7)))
    )
    step = whole.astype(jnp.int32) & 3
    swap = (step & 1) == 1
    cos_base = jnp.where(swap, sine, cosine)
    sin_base = jnp.where(swap, cosine, sine)
    cos_value = jnp.where((step == 1) | (step == 2), -cos_base, cos_base)
    sin_value = jnp.where(step >= 2, -sin_base, sin_base)
    return cos_value, sin_value


def turns_of(product, length, inverse):
    whole = jnp.round(product * inverse)
    return (product - whole * length) * inverse


def grid_kernel(len_ref, inv_ref, order_lane_ref, order_sub_ref, row_ref, grid_ref, back_ref):
    lane_f = lax.broadcasted_iota(jnp.int32, (ROWS_PAD, LANES), 1)
    row_f = lax.broadcasted_iota(jnp.int32, (ROWS_PAD, LANES), 0)
    block_start = (row_f // 2) * LANES
    position = block_start + lane_f
    block_start = block_start.astype(jnp.float32)
    second_lane = (lax.broadcasted_iota(jnp.int32, (1, LANES), 1) // SLOT_PAD) % 2 == 1
    sign = jnp.where(lax.broadcasted_iota(jnp.int32, (1, LANES), 1) < 64, 1.0, -1.0)
    order_lane = order_lane_ref[0:1, :]
    inner_lane = lax.broadcasted_iota(jnp.int32, (SLOT_PAD, LANES), 1).astype(jnp.float32)
    inner_product = order_sub_ref[...] * inner_lane
    north = (lax.broadcasted_iota(jnp.int32, (ROWS_PAD, LANES), 0) % 2) == 0
    zero_block = jnp.zeros((SLOT_PAD, LANES), jnp.bfloat16)

    def one_row(row):
        first = len_ref[row, 0]
        second = len_ref[row, 1]
        first_f = first.astype(jnp.float32)
        second_f = second.astype(jnp.float32)
        inv_first = inv_ref[row, 0]
        inv_second = inv_ref[row, 1]
        length_lane = jnp.where(second_lane, second_f, first_f)
        inverse_lane = jnp.where(second_lane, inv_second, inv_first)
        start_lane = jnp.where(second_lane, first_f, 0.0)
        outer = order_lane * (block_start - start_lane)
        outer_cos, outer_sin = cos_sin_turns(turns_of(outer, length_lane, inverse_lane))
        cos_a, sin_a = cos_sin_turns(turns_of(inner_product, first_f, inv_first))
        cos_b, sin_b = cos_sin_turns(turns_of(inner_product, second_f, inv_second))
        inner = jnp.concatenate(
            [
                jnp.concatenate([cos_a.astype(jnp.bfloat16), zero_block], 1),
                jnp.concatenate([zero_block, cos_b.astype(jnp.bfloat16)], 1),
                jnp.concatenate([(-sin_a).astype(jnp.bfloat16), zero_block], 1),
                jnp.concatenate([zero_block, (-sin_b).astype(jnp.bfloat16)], 1),
            ],
            0,
        )
        waves = row_ref[row]
        plain = jnp.where(north, waves[0:1, :], waves[1:2, :])
        crossed = jnp.where(north, waves[2:3, :], waves[3:4, :])
        spread = (plain * outer_cos + crossed * outer_sin).astype(jnp.bfloat16)
        images = lax.dot_general(
            spread, inner, (((1,), (0,)), ((), ())), preferred_element_type=jnp.float32
        )
        in_first = position < first
        occupied = position < first + second
        values = jnp.where(in_first, images[:, :LANES], jnp.where(occupied, images[:, LANES:], 0.0))
        values = values.astype(jnp.bfloat16)
        wide = values.astype(jnp.float32)
        squared = wide * wide
        by_cycle = jnp.concatenate(
            [
                jnp.where(in_first, squared, 0.0).astype(jnp.bfloat16),
                jnp.where(in_first, 0.0, squared).astype(jnp.bfloat16),
            ],
            1,
        )
        partial = lax.dot_general(
            by_cycle, inner, (((1,), (1,)), ((), ())), preferred_element_type=jnp.float32
        )
        cos_sum = jnp.sum((partial * outer_cos).reshape(ROWS_PAD // 8, 8, LANES), 0)
        sin_sum = jnp.sum((partial * outer_sin).reshape(ROWS_PAD // 8, 8, LANES), 0)
        total = cos_sum + sign * pltpu.roll(sin_sum, 64, 1)
        total = total + pltpu.roll(total, 4, 0)
        total = total + pltpu.roll(total, 2, 0)
        back_ref[row] = total * waves[4:5, :]
        return values

    @pl.loop(0, len_ref.shape[0] // 2)
    def _(pair):
        even = one_row(2 * pair)
        odd = one_row(2 * pair + 1)
        start = pl.multiple_of(pair * 2 * ROWS, 8)
        grid_ref[pl.ds(start, 2 * ROWS), :] = jnp.concatenate([even[:ROWS], odd[:ROWS]], 0)


def per_device(spec, legendre, gauss_w, cycle_len, wave_map):
    slots_dev = spec.shape[0]
    fields = spec.shape[1]
    degrees_all = spec.shape[3]
    slot_count = wave_map.shape[0]
    orders = wave_map * degrees_all // slot_count
    wave_pos = lax.axis_index("wave")
    own_orders = lax.dynamic_slice_in_dim(orders, wave_pos * slots_dev, slots_dev)
    degrees = jnp.arange(degrees_all, dtype=jnp.int32)
    retained = degrees[None, :] >= own_orders[:, None]
    coefficients = jnp.where(retained[:, None, None, :], spec, jnp.zeros((), jnp.bfloat16))
    panels = lax.all_gather(legendre, "lev", axis=1, tiled=True)
    sign_flip = parity_of(degrees, own_orders)
    flipped = (coefficients.astype(jnp.float32) * sign_flip[:, None, None, :]).astype(jnp.bfloat16)
    stacked = jnp.stack([coefficients, flipped], 1)
    fourier = jnp.einsum(
        "shfcn,snq->shfcq", stacked, panels, preferred_element_type=jnp.float32
    ).astype(jnp.bfloat16)
    cycle_waves = lax.all_to_all(fourier, "wave", split_axis=4, concat_axis=0, tiled=True)
    local_lats = cycle_waves.shape[4]
    row_total = local_lats // 2
    lat_start = wave_pos * local_lats
    lens = lax.dynamic_slice_in_dim(cycle_len, lat_start, local_lats).reshape(row_total, 2)
    weights = lax.dynamic_slice_in_dim(gauss_w, lat_start, local_lats).reshape(row_total, 2)
    double = jnp.where(orders == 0, 1.0, 2.0)
    resolved = 2 * orders[None, None, :] < lens[:, :, None]
    widening = jnp.where(resolved, double[None, None, :], 0.0)
    waves = cycle_waves.reshape(slot_count, 2, 2, row_total, 2).transpose(3, 1, 2, 4, 0)
    waves = waves.astype(jnp.float32) * widening[:, None, None, :, :]
    crossed = jnp.stack([-waves[:, :, 1], waves[:, :, 0]], 2)
    factor = jnp.where(resolved, weights[:, :, None] / lens[:, :, None].astype(jnp.float32), 0.0)
    factor = jnp.broadcast_to(factor[:, None, None], (row_total, 1, 2, 2, slot_count))
    rows = jnp.concatenate([waves, crossed, factor, jnp.zeros((row_total, 3, 2, 2, slot_count), jnp.float32)], 1)
    spare = SLOT_PAD - slot_count
    rows = jnp.pad(rows, ((0, 0), (0, 0), (0, 0), (0, 0), (0, spare))).reshape(row_total, 8, LANES)
    padded_orders = jnp.pad(orders.astype(jnp.float32), (0, spare))
    order_lane = jnp.broadcast_to(jnp.tile(padded_orders, 4)[None, :], (8, LANES))
    order_sub = jnp.broadcast_to(padded_orders[:, None], (SLOT_PAD, LANES))
    inverse = 1.0 / lens.astype(jnp.float32)
    smem = pl.BlockSpec(memory_space=pltpu.SMEM)
    vmem = pl.BlockSpec(memory_space=pltpu.VMEM)
    values, back = pl.pallas_call(
        grid_kernel,
        out_shape=(
            jax.ShapeDtypeStruct((row_total * ROWS, LANES), jnp.bfloat16),
            jax.ShapeDtypeStruct((row_total, 8, LANES), jnp.float32),
        ),
        in_specs=[smem, smem, vmem, vmem, vmem],
        out_specs=(vmem, vmem),
        name="cycles",
    )(lens, inverse, order_lane, order_sub, rows)
    grid = values.reshape(row_total, BLOCKS, 2, LANES).transpose(2, 0, 1, 3)
    grid = grid.reshape(2, row_total, 1, LPAD)
    returned = back[:, :2].reshape(row_total, 2, 2, 2, SLOT_PAD)[..., :slot_count].astype(jnp.bfloat16)
    returned = returned.transpose(4, 1, 2, 0, 3).reshape(slot_count, 2, fields, 2, local_lats)
    spectral = lax.all_to_all(returned, "wave", split_axis=0, concat_axis=4, tiled=True)
    both = jnp.einsum("shfcq,snq->shfcn", spectral, panels, preferred_element_type=jnp.float32)
    total = both[:, 0] + sign_flip[:, None, None, :] * both[:, 1]
    spec_out = jnp.where(retained[:, None, None, :], total, 0.0)
    return (grid, spec_out)


def solution(mesh):
    placed = (P("wave", "lev", None, None), P("wave", "lev", None), P(), P(), P())
    return jax.shard_map(
        per_device,
        mesh=mesh,
        in_specs=placed,
        out_specs=(P(None, "wave", "lev", None), P("wave", "lev", None, None)),
        check_vma=False,
    )
```

time: 551 us -> 191 us (0.35)
  other arithmetic: 342 us -> 3.76 us
  matrix products: 36 us -> 8.55 us
  Pallas kernels: 0 us -> 16.6 us
  blocking collectives: 11.8 us -> 0 us
  local copies, waits for them, and re-layouts: 25.8 us -> 19.1 us
    convert_element_type x20 -> x0, other arithmetic: 329 us -> none  [the longest x5 320 us: cycle_tables(): jnp.where(occupied[:, None, :], jnp.cos(angles), 0.0).astype(jnp.bfloat16)]
    dot_general x10 -> x0, matrix products: 27.5 us -> none  [the longest x5 15.5 us: cycle_block(): jnp.einsum('rap,rkp->rak', by_cycle, tables, preferred_element_type=jnp.f...]
    pallas_call x0 -> x1, Pallas kernels: none -> 16.6 us  [per_device(): pl.pallas_call(grid_kernel, out_shape=(jax.ShapeDtypeStruct((row_total *...]
    all_to_all x1 -> x0, blocking collectives: 11.8 us -> none  [per_device(): lax.all_to_all(returned, 'wave', split_axis=0, concat_axis=4, tiled=True)]
    all_to_all x0 -> x1, waiting for transfers between devices: none -> 5.88 us  [per_device(): lax.all_to_all(returned, 'wave', split_axis=0, concat_axis=4, tiled=True)]
  transfers between devices with their start and end apart: 2 -> 3, of which waited for: 2 -> 3; matrix products, arithmetic and copies ran while one was open for 1% -> 4% of each run, Pallas kernels for 0% -> 0%
where the time goes in v1:
time: 191 us; the launch traced here: 190 us
  waiting for transfers between devices  114 us (60%)
  local copies, waits for them, and re-layouts  19.1 us (10%)
  Pallas kernels  16.6 us (9%)
  between operations  14.2 us (7%)
  starting transfers between devices  13.4 us (7%)
  matrix products  8.55 us (4%)
  other arithmetic  3.76 us (2%)
    all_gather x1, waiting for transfers between devices, per_device(): panels = lax.all_gather(legendre, 'lev', axis=1, tiled=True)  98.6 us
    pallas_call x1, Pallas kernels, per_device(): pl.pallas_call(grid_kernel, out_shape=(jax.ShapeDtypeStruct((row_total *...  16.6 us
    all_to_all x1, starting transfers between devices, per_device(): lax.all_to_all(fourier, 'wave', split_axis=4, concat_axis=0, tiled=True)  9.9 us
    all_to_all x1, waiting for transfers between devices, per_device(): lax.all_to_all(fourier, 'wave', split_axis=4, concat_axis=0, tiled=True)  9.03 us
    all_to_all x1, waiting for transfers between devices, per_device(): lax.all_to_all(returned, 'wave', split_axis=0, concat_axis=4, tiled=True)  5.88 us
    dot_general x1, matrix products, per_device(): jnp.einsum('shfcq,snq->shfcn', spectral, panels, preferred_element_type=j...  4.69 us
    dot_general x1, matrix products, per_device(): jnp.einsum('shfcn,snq->shfcq', stacked, panels, preferred_element_type=jn...  3.86 us
  transfers between devices with their start and end apart: 3, of which 3 were waited for; matrix products, arithmetic and copies ran while one was open for 4% of the time, Pallas kernels for 0%

profile of v1, /device:TPU:1, one launch (start us, length us, event | category | flops | bytes accessed | tf_op | source)
XLA Modules:
  0.0 189.9 jit_solution(9122318427577053298)
XLA Ops:
  7.2 0.7 all-gather.2.cloned.1.call-update
  7.9 0.8 dynamic_slice.9
  8.8 0.8 dynamic_slice.11
  9.6 0.1 broadcast_in_dim_reshape.2
  9.8 0.6 convert_divide_fusion
  10.5 0.7 compare_select_fusion.5
  11.4 0.7 fusion.22
  12.2 0.7 fusion.20
  12.9 98.6 %all-gather.2.cloned.1.call-done = bf16[2,1280,1200]{2,0,1:T(2,128)(2,1)} async-done(((bf16[2,20,1200]{2,0,1:T(2,128)(2,1)}), bf16[2,1280,1200]{2,0,1:T(2,128)(2,1)}) %all-gather.2.cloned.1.call-update) | async-done | bytes 6144016 | tf_op jit(solution)/shard_map/all_gather | solution.py:134
  111.5 3.9 %fusion.11 = bf16[2,2,1,2,1200]{4,3,1,0,2:T(2,128)(2,1)S(1)} fusion(bf16[2,1280,1200,1]{2,0,1,3:T(2,128)(2,1)} %bitcast.66, bf16[2,1,1,2,1280]{4,3,1,0,2:T(2,128)(2,1)S(1)} %fusion.20, bf16[2,1,1,2,1280]{4,3,1,0,2:T(2,128)(2,1)S(1)} %fusion.22), kind=kOutput, calls=%fused_computation.7 | convolution fusion | flops 24626560 | bytes 6183680 | tf_op jit(solution)/shard_map/shfcn,snq->shfcq/dot_general | solution.py:138
  115.4 2.6 %copy.53 = bf16[2,2,1,2,1200]{3,1,0,2,4:T(2,128)(2,1)S(1)} copy(bf16[2,2,1,2,1200]{4,3,1,0,2:T(2,128)(2,1)S(1)} %fusion.11) | data formatting | bytes 38400 | tf_op jit(solution)/shard_map/convert_element_type | solution.py:140
  118.0 1.7 reshape.155
  119.7 9.9 %all-to-all-start = ((bf16[12,2,400]{2,1,0:T(2,128)(2,1)}), bf16[12,2,400]{2,1,0:T(2,128)(2,1)S(1)}, u32[]{:S(2)}, u32[]{:S(2)}) async-start(bf16[12,2,400]{2,1,0:T(2,128)(2,1)} %reshape.155), calls=%async_computation | async-start | bytes 49152 | tf_op jit(solution)/shard_map/all_to_all | solution.py:141
  129.8 9.0 %all-to-all-done = bf16[12,2,400]{2,1,0:T(2,128)(2,1)S(1)} async-done(((bf16[12,2,400]{2,1,0:T(2,128)(2,1)}), bf16[12,2,400]{2,1,0:T(2,128)(2,1)S(1)}, u32[]{:S(2)}, u32[]{:S(2)}) %all-to-all-start) | async-done | bytes 19232 | tf_op jit(solution)/shard_map/all_to_all | solution.py:141
  138.9 0.8 reshape.156
  139.7 2.4 %copy.54 = bf16[2,2,1,2,1200]{4,3,2,1,0:T(2,128)(2,1)S(1)} copy(bf16[2,2,1,2,1200]{3,1,0,2,4:T(2,128)(2,1)S(1)} %bitcast.68) | data formatting | bytes 38400 | tf_op jit(solution)/shard_map/all_to_all | solution.py:141
  142.2 0.8 reshape.150
  143.0 1.0 copy.56
  144.2 0.9 copy.59.row_ref
  145.1 0.7 broadcast_in_dim.95.order_sub_ref
  145.8 0.6 broadcast_in_dim.94.order_lane_ref
  146.4 16.6 %cycles.1 = (bf16[3800,128]{1,0:T(8,128)(2,1)}, f32[50,8,128]{2,1,0:T(8,128)}) custom-call(s32[50,2]{1,0:T(8,128)} %copy-done, f32[50,2]{1,0:T(8,128)} %get-tuple-element.19.inv_ref, f32[8,128]{1,0:T(8,128)} %broadcast_in_dim.94.order_lane_ref, f32[32,128]{1,0:T(8,128)} %broadcast_in_dim.95.order_sub_ref, f32[50,8,128]{2,1,0:T(8,128)} %copy.59.row_ref), custom_call_target="tpu_custom_call" | custom-call | tf_op jit(solution)/shard_map/cycles/pallas_call | solution.py:164
  162.9 0.9 slice.47
  163.9 0.1 copy.61
  164.0 0.1 copy.62
  164.2 0.7 copy.63
  164.9 3.4 %all-to-all-start.1 = ((bf16[24,2,1,2,100]{4,3,2,1,0:T(2,128)(2,1)}), bf16[24,2,1,2,100]{4,3,2,1,0:T(2,128)(2,1)S(1)}, u32[]{:S(2)}, u32[]{:S(2)}) async-start(bf16[24,2,1,2,100]{4,3,2,1,0:T(2,128)(2,1)} %copy.63), calls=%async_computation.1 | async-start | bytes 49152 | tf_op jit(solution)/shard_map/all_to_all | solution.py:178
  168.4 1.3 copy.90
  169.7 2.0 %reshape.146 = bf16[2,50,1,4864]{3,0,1,2:T(2,128)(2,1)} reshape(bf16[2,50,38,128]{3,2,0,1:T(8,128)(2,1)S(1)} %bitcast.69) | data formatting | bytes 1945600 | tf_op jit(solution)/shard_map/reshape | solution.py:175
  171.7 5.9 %all-to-all-done.1 = bf16[24,2,1,2,100]{4,3,2,1,0:T(2,128)(2,1)S(1)} async-done(((bf16[24,2,1,2,100]{4,3,2,1,0:T(2,128)(2,1)}), bf16[24,2,1,2,100]{4,3,2,1,0:T(2,128)(2,1)S(1)}, u32[]{:S(2)}, u32[]{:S(2)}) %all-to-all-start.1) | async-done | bytes 19232 | tf_op jit(solution)/shard_map/all_to_all | solution.py:178
  177.7 4.7 %fusion.5 = f32[2,2,1,2,1280]{4,3,0,2,1:T(2,128)S(1)} fusion(bf16[2,2,2,1200]{3,2,0,1:T(2,128)(2,1)S(1)} %reshape.154, bf16[2,1280,1200]{2,0,1:T(2,128)(2,1)} %all-gather.2.cloned.1.call-done), kind=kOutput, calls=%fused_computation.5 | convolution fusion | flops 24576000 | bytes 6204160 | tf_op jit(solution)/shard_map/shfcq,snq->shfcn/dot_general | solution.py:179
  182.4 0.6 fusion.17
  (27 shorter events, 1.3 us)
Async XLA Ops:
  7.2 104.4 %all-gather.2.cloned.1.call-start = ((), (), s32[]{:S(2)}) async-start(), calls=%async_computation.2 | async-start | bytes 6656000 | tf_op jit(solution)/shard_map/all_gather | solution.py:134
  8.8 134.2 %copy-start = (s32[50,2]{1,0:T(8,128)}, s32[50,2]{1,0:T(8,128)S(1)}, u32[]{:S(2)}) copy-start(s32[50,2]{1,0:T(8,128)S(1)} %reshape.142.len_ref) | copy-start | bytes 1204
  119.7 19.2 %all-to-all-start = ((bf16[12,2,400]{2,1,0:T(2,128)(2,1)}), bf16[12,2,400]{2,1,0:T(2,128)(2,1)S(1)}, u32[]{:S(2)}, u32[]{:S(2)}) async-start(bf16[12,2,400]{2,1,0:T(2,128)(2,1)} %reshape.155), calls=%async_computation | async-start | bytes 49152 | tf_op jit(solution)/shard_map/all_to_all | solution.py:141
  164.9 12.7 %all-to-all-start.1 = ((bf16[24,2,1,2,100]{4,3,2,1,0:T(2,128)(2,1)}), bf16[24,2,1,2,100]{4,3,2,1,0:T(2,128)(2,1)S(1)}, u32[]{:S(2)}, u32[]{:S(2)}) async-start(bf16[24,2,1,2,100]{4,3,2,1,0:T(2,128)(2,1)} %copy.63), calls=%async_computation.1 | async-start | bytes 49152 | tf_op jit(solution)/shard_map/all_to_all | solution.py:178
Sparse Core Ops, SparseCore 0:
  11.8 99.6 all-gather.1

commit v2 on v1

--- a/solution.py
+++ b/solution.py
@@ -2,6 +2,7 @@
 
 import jax
 import jax.numpy as jnp
+import numpy as np
 from jax import lax
 from jax.experimental import pallas as pl
 from jax.experimental.pallas import tpu as pltpu
@@ -13,10 +14,13 @@
 ROWS = 2 * BLOCKS
 ROWS_PAD = 80
 SLOT_PAD = 32
-
-
-def parity_of(degree_ids, own_orders):
-    return jnp.where((degree_ids[None, :] + own_orders[:, None]) % 2 == 0, 1.0, -1.0)
+CYCLE_PAD = 64
+WAVES = 12
+LINES = 8
+LEAF = 8
+LATS = WAVES * LANES
+MESH = pl.DeviceIdType.MESH
+NT = (((1,), (1,)), ((), ()))
 
 
 def cos_sin_turns(turns):
@@ -44,7 +48,163 @@
     return (product - whole * length) * inverse
 
 
-def grid_kernel(len_ref, inv_ref, order_lane_ref, order_sub_ref, row_ref, grid_ref, back_ref):
+def where_am_i():
+    wave = lax.axis_index("wave")
+    lev = lax.axis_index("lev")
+    line = lax.div(lev, LEAF)
+    leaf = lax.rem(lev, LEAF)
+    return wave, lev, line, leaf
+
+
+def remote(source, target, send, receive, device):
+    return pltpu.make_async_remote_copy(
+        src_ref=source, dst_ref=target, send_sem=send, recv_sem=receive,
+        device_id=device, device_id_type=MESH,
+    )
+
+
+def greet(devices):
+    barrier = pltpu.get_barrier_semaphore()
+    for device in devices:
+        pl.semaphore_signal(barrier, inc=1, device_id=device, device_id_type=MESH)
+    pl.semaphore_wait(barrier, len(devices))
+
+
+def front_kernel(
+    leg_ref, coef_ref, panel_ref, waves_ref, lhs, part, got, four,
+    local_sem, chip_send, chip_recv, core_send, core_recv, coef_send, coef_recv,
+    part_send, part_recv, wave_send, wave_recv,
+):
+    wave, lev, line, leaf = where_am_i()
+    core = lax.rem(leaf, 2)
+    chip = lax.div(leaf, 2)
+    sibling = {"lev": lev + 1 - 2 * core}
+    chips = [{"lev": line * LEAF + lax.rem(chip + d, 4) * 2 + core} for d in range(1, 4)]
+    lines = [{"lev": lax.rem(line + d, LINES) * LEAF + leaf} for d in range(1, LINES)]
+    waves = [{"wave": lax.rem(wave + d, WAVES)} for d in range(1, WAVES)]
+    greet([sibling] + chips + lines + waves)
+
+    copies = []
+    for d in range(1, 4):
+        copy = remote(leg_ref, panel_ref.at[leaf], chip_send.at[d - 1], chip_recv.at[d - 1], chips[d - 1])
+        copy.start()
+        copies.append(copy)
+    for d in range(1, LINES):
+        target = lax.rem(line + d, LINES)
+        copy = remote(coef_ref.at[target], lhs.at[line], coef_send.at[d - 1], coef_recv.at[d - 1], lines[d - 1])
+        copy.start()
+        copies.append(copy)
+    copy = remote(leg_ref, panel_ref.at[leaf], core_send.at[0], core_recv.at[0], sibling)
+    copy.start()
+    copies.append(copy)
+    own_panel = pltpu.make_async_copy(leg_ref, panel_ref.at[leaf], local_sem.at[0])
+    own_panel.start()
+    own_coef = pltpu.make_async_copy(coef_ref.at[line], lhs.at[line], local_sem.at[1])
+    own_coef.start()
+    for d in range(1, 4):
+        origin = lax.rem(chip + 4 - d, 4) * 2 + core
+        block = panel_ref.at[origin]
+        remote(block, block, chip_send.at[d - 1], chip_recv.at[d - 1], chips[d - 1]).wait_recv()
+        copy = remote(block, block, core_send.at[d], core_recv.at[d], sibling)
+        copy.start()
+        copies.append(copy)
+    own_panel.wait()
+    own_coef.wait()
+    for d in range(4):
+        origin = lax.rem(chip + 4 - d, 4) * 2 + 1 - core
+        block = panel_ref.at[origin]
+        remote(block, block, core_send.at[d], core_recv.at[d], sibling).wait_recv()
+    for d in range(1, LINES):
+        block = lhs.at[lax.rem(line + LINES - d, LINES)]
+        remote(block, block, coef_send.at[d - 1], coef_recv.at[d - 1], lines[d - 1]).wait_recv()
+
+    depth = panel_ref.shape[1]
+    panel = panel_ref[...].reshape(LEAF * depth, LATS)
+    product = jnp.dot(
+        lhs[...].reshape(LINES * 8, LEAF * depth), panel, preferred_element_type=jnp.float32
+    )
+    part[...] = product.reshape(LINES, 8, LATS)
+    for d in range(1, LINES):
+        target = lax.rem(line + d, LINES)
+        copy = remote(part.at[target], got.at[d - 1], part_send.at[d - 1], part_recv.at[d - 1], lines[d - 1])
+        copy.start()
+        copies.append(copy)
+    total = part[line]
+    for d in range(1, LINES):
+        block = got.at[d - 1]
+        remote(block, block, part_send.at[d - 1], part_recv.at[d - 1], lines[d - 1]).wait_recv()
+        total = total + got[d - 1]
+    for w in range(WAVES):
+        four[w] = total[:, w * LANES : (w + 1) * LANES].astype(jnp.bfloat16)
+    for d in range(1, WAVES):
+        target = lax.rem(wave + d, WAVES)
+        copy = remote(four.at[target], waves_ref.at[wave], wave_send.at[d - 1], wave_recv.at[d - 1], waves[d - 1])
+        copy.start()
+        copies.append(copy)
+    own_wave = pltpu.make_async_copy(four.at[wave], waves_ref.at[wave], local_sem.at[2])
+    own_wave.start()
+    own_wave.wait()
+    for d in range(1, WAVES):
+        block = waves_ref.at[lax.rem(wave + WAVES - d, WAVES)]
+        remote(block, block, wave_send.at[d - 1], wave_recv.at[d - 1], waves[d - 1]).wait_recv()
+    for copy in copies:
+        copy.wait_send()
+
+
+def back_kernel(
+    ret_ref, panel_ref, out_ref, here, fields, part,
+    local_sem, wave_send, wave_recv, line_send, line_recv, part_send, part_recv,
+):
+    wave, lev, line, leaf = where_am_i()
+    lines = [{"lev": lax.rem(line + d, LINES) * LEAF + leaf} for d in range(1, LINES)]
+    waves = [{"wave": lax.rem(wave + d, WAVES)} for d in range(1, WAVES)]
+    greet(lines + waves)
+    copies = []
+    for d in range(1, WAVES):
+        target = lax.rem(wave + d, WAVES)
+        copy = remote(ret_ref.at[target], here.at[wave], wave_send.at[d - 1], wave_recv.at[d - 1], waves[d - 1])
+        copy.start()
+        copies.append(copy)
+    own_wave = pltpu.make_async_copy(ret_ref.at[wave], here.at[wave], local_sem.at[0])
+    own_wave.start()
+    own_wave.wait()
+    for d in range(1, WAVES):
+        block = here.at[lax.rem(wave + WAVES - d, WAVES)]
+        remote(block, block, wave_send.at[d - 1], wave_recv.at[d - 1], waves[d - 1]).wait_recv()
+    for d in range(1, LINES):
+        copy = remote(here, fields.at[line], line_send.at[d - 1], line_recv.at[d - 1], lines[d - 1])
+        copy.start()
+        copies.append(copy)
+    own_line = pltpu.make_async_copy(here, fields.at[line], local_sem.at[1])
+    own_line.start()
+    own_line.wait()
+    for d in range(1, LINES):
+        block = fields.at[lax.rem(line + LINES - d, LINES)]
+        remote(block, block, line_send.at[d - 1], line_recv.at[d - 1], lines[d - 1]).wait_recv()
+    depth = panel_ref.shape[1]
+    panel = panel_ref[...].reshape(LEAF * depth, LATS)
+    lhs = jnp.concatenate([fields[:, w].reshape(LINES * 8, LANES) for w in range(WAVES)], 1)
+    product = lax.dot_general(lhs, panel, NT, preferred_element_type=jnp.float32)
+    part[...] = product.reshape(LINES, 8, LEAF * depth)
+    for d in range(1, LINES):
+        target = lax.rem(line + d, LINES)
+        copy = remote(part.at[target], out_ref.at[line], part_send.at[d - 1], part_recv.at[d - 1], lines[d - 1])
+        copy.start()
+        copies.append(copy)
+    own_part = pltpu.make_async_copy(part.at[line], out_ref.at[line], local_sem.at[2])
+    own_part.start()
+    own_part.wait()
+    for d in range(1, LINES):
+        block = out_ref.at[lax.rem(line + LINES - d, LINES)]
+        remote(block, block, part_send.at[d - 1], part_recv.at[d - 1], lines[d - 1]).wait_recv()
+    for copy in copies:
+        copy.wait_send()
+
+
+def grid_kernel(
+    len_ref, inv_ref, order_lane_ref, order_sub_ref, keep_ref, factor_ref, wave_ref, spread_ref, gather_ref,
+    grid_ref, ret_ref, plain_ref, cross_ref, sum_ref,
+):
     lane_f = lax.broadcasted_iota(jnp.int32, (ROWS_PAD, LANES), 1)
     row_f = lax.broadcasted_iota(jnp.int32, (ROWS_PAD, LANES), 0)
     block_start = (row_f // 2) * LANES
@@ -56,6 +216,16 @@
     inner_lane = lax.broadcasted_iota(jnp.int32, (SLOT_PAD, LANES), 1).astype(jnp.float32)
     inner_product = order_sub_ref[...] * inner_lane
     north = (lax.broadcasted_iota(jnp.int32, (ROWS_PAD, LANES), 0) % 2) == 0
+    arrived = wave_ref[...].reshape(WAVES * 8, LANES)
+    turned = lax.dot_general(
+        arrived, spread_ref[...], (((0,), (0,)), ((), ())), preferred_element_type=jnp.float32
+    )
+    for h in range(2):
+        part = turned[:, h * LANES : (h + 1) * LANES]
+        part = jnp.where(second_lane, part[CYCLE_PAD:], part[:CYCLE_PAD]) * keep_ref[...]
+        plain_ref[h] = part
+        cross_ref[h] = -sign * pltpu.roll(part, 64, 1)
+    sum_ref[...] = jnp.zeros_like(sum_ref)
     zero_block = jnp.zeros((SLOT_PAD, LANES), jnp.bfloat16)
 
     def one_row(row):
@@ -81,9 +251,8 @@
             ],
             0,
         )
-        waves = row_ref[row]
-        plain = jnp.where(north, waves[0:1, :], waves[1:2, :])
-        crossed = jnp.where(north, waves[2:3, :], waves[3:4, :])
+        plain = jnp.where(north, plain_ref[0, pl.ds(row, 1), :], plain_ref[1, pl.ds(row, 1), :])
+        crossed = jnp.where(north, cross_ref[0, pl.ds(row, 1), :], cross_ref[1, pl.ds(row, 1), :])
         spread = (plain * outer_cos + crossed * outer_sin).astype(jnp.bfloat16)
         images = lax.dot_general(
             spread, inner, (((1,), (0,)), ((), ())), preferred_element_type=jnp.float32
@@ -109,7 +278,8 @@
         total = cos_sum + sign * pltpu.roll(sin_sum, 64, 1)
         total = total + pltpu.roll(total, 4, 0)
         total = total + pltpu.roll(total, 2, 0)
-        back_ref[row] = total * waves[4:5, :]
+        sum_ref[0, pl.ds(row, 1), :] = total[0:1, :]
+        sum_ref[1, pl.ds(row, 1), :] = total[1:2, :]
         return values
 
     @pl.loop(0, len_ref.shape[0] // 2)
@@ -119,65 +289,128 @@
         start = pl.multiple_of(pair * 2 * ROWS, 8)
         grid_ref[pl.ds(start, 2 * ROWS), :] = jnp.concatenate([even[:ROWS], odd[:ROWS]], 0)
 
+    sums = jnp.concatenate([sum_ref[0] * factor_ref[...], sum_ref[1] * factor_ref[...]], 1).astype(jnp.bfloat16)
+    returned = jnp.concatenate(
+        [
+            lax.dot_general(gather_ref[cycle], sums, NT, preferred_element_type=jnp.float32)
+            for cycle in range(2)
+        ],
+        1,
+    )
+    ret_ref[...] = returned.astype(jnp.bfloat16).reshape(WAVES, 8, LANES)
 
 def per_device(spec, legendre, gauss_w, cycle_len, wave_map):
-    slots_dev = spec.shape[0]
-    fields = spec.shape[1]
-    degrees_all = spec.shape[3]
+    slots_dev, _, _, degrees_all = spec.shape
+    depth = legendre.shape[1]
     slot_count = wave_map.shape[0]
     orders = wave_map * degrees_all // slot_count
     wave_pos = lax.axis_index("wave")
     own_orders = lax.dynamic_slice_in_dim(orders, wave_pos * slots_dev, slots_dev)
     degrees = jnp.arange(degrees_all, dtype=jnp.int32)
+    local_lats = cycle_len.shape[0] // WAVES
+    row_total = local_lats // 2
+    spare = SLOT_PAD - slot_count
+
+    panel = legendre.transpose(1, 0, 2).reshape(depth * slots_dev, WAVES, row_total, 2).transpose(0, 1, 3, 2)
+    panel = jnp.pad(panel, ((0, 0), (0, 0), (0, 0), (0, CYCLE_PAD - row_total))).reshape(depth * slots_dev, LATS)
+
     retained = degrees[None, :] >= own_orders[:, None]
-    coefficients = jnp.where(retained[:, None, None, :], spec, jnp.zeros((), jnp.bfloat16))
-    panels = lax.all_gather(legendre, "lev", axis=1, tiled=True)
-    sign_flip = parity_of(degrees, own_orders)
-    flipped = (coefficients.astype(jnp.float32) * sign_flip[:, None, None, :]).astype(jnp.bfloat16)
-    stacked = jnp.stack([coefficients, flipped], 1)
-    fourier = jnp.einsum(
-        "shfcn,snq->shfcq", stacked, panels, preferred_element_type=jnp.float32
-    ).astype(jnp.bfloat16)
-    cycle_waves = lax.all_to_all(fourier, "wave", split_axis=4, concat_axis=0, tiled=True)
-    local_lats = cycle_waves.shape[4]
-    row_total = local_lats // 2
+    odd = (degrees[None, :] + own_orders[:, None]) % 2 == 1
+    coefficients = jnp.where(retained[:, None, :], spec[:, 0], jnp.zeros((), jnp.bfloat16))
+    flipped = jnp.where(odd[:, None, :], -coefficients, coefficients)
+    stacked = jnp.stack([coefficients, flipped], 1).reshape(slots_dev, 4, LINES, degrees_all // LINES, 1)
+    same = jnp.arange(slots_dev)[:, None, None, None, None] == jnp.arange(slots_dev)
+    coef = jnp.where(same, stacked, jnp.zeros((), jnp.bfloat16)).transpose(2, 0, 1, 3, 4)
+    coef = coef.reshape(LINES, 8, degrees_all // LINES * slots_dev)
+
+    vmem = pl.BlockSpec(memory_space=pltpu.VMEM)
+    smem = pl.BlockSpec(memory_space=pltpu.SMEM)
+    dma = pltpu.SemaphoreType.DMA
+    width = LEAF * depth * slots_dev
+    panels, arrived = pl.pallas_call(
+        front_kernel,
+        out_shape=(
+            jax.ShapeDtypeStruct((LEAF, depth * slots_dev, LATS), jnp.bfloat16),
+            jax.ShapeDtypeStruct((WAVES, 8, LANES), jnp.bfloat16),
+        ),
+        in_specs=[vmem, vmem],
+        out_specs=(vmem, vmem),
+        scratch_shapes=[
+            pltpu.VMEM((LINES, 8, width), jnp.bfloat16),
+            pltpu.VMEM((LINES, 8, LATS), jnp.float32),
+            pltpu.VMEM((LINES - 1, 8, LATS), jnp.float32),
+            pltpu.VMEM((WAVES, 8, LANES), jnp.bfloat16),
+            dma((3,)), dma((3,)), dma((3,)), dma((4,)), dma((4,)),
+            dma((LINES - 1,)), dma((LINES - 1,)), dma((LINES - 1,)), dma((LINES - 1,)),
+            dma((WAVES - 1,)), dma((WAVES - 1,)),
+        ],
+        compiler_params=pltpu.CompilerParams(collective_id=0, has_side_effects=True),
+        name="front",
+    )(panel, coef)
+
     lat_start = wave_pos * local_lats
     lens = lax.dynamic_slice_in_dim(cycle_len, lat_start, local_lats).reshape(row_total, 2)
     weights = lax.dynamic_slice_in_dim(gauss_w, lat_start, local_lats).reshape(row_total, 2)
-    double = jnp.where(orders == 0, 1.0, 2.0)
-    resolved = 2 * orders[None, None, :] < lens[:, :, None]
-    widening = jnp.where(resolved, double[None, None, :], 0.0)
-    waves = cycle_waves.reshape(slot_count, 2, 2, row_total, 2).transpose(3, 1, 2, 4, 0)
-    waves = waves.astype(jnp.float32) * widening[:, None, None, :, :]
-    crossed = jnp.stack([-waves[:, :, 1], waves[:, :, 0]], 2)
-    factor = jnp.where(resolved, weights[:, :, None] / lens[:, :, None].astype(jnp.float32), 0.0)
-    factor = jnp.broadcast_to(factor[:, None, None], (row_total, 1, 2, 2, slot_count))
-    rows = jnp.concatenate([waves, crossed, factor, jnp.zeros((row_total, 3, 2, 2, slot_count), jnp.float32)], 1)
-    spare = SLOT_PAD - slot_count
-    rows = jnp.pad(rows, ((0, 0), (0, 0), (0, 0), (0, 0), (0, spare))).reshape(row_total, 8, LANES)
-    padded_orders = jnp.pad(orders.astype(jnp.float32), (0, spare))
-    order_lane = jnp.broadcast_to(jnp.tile(padded_orders, 4)[None, :], (8, LANES))
-    order_sub = jnp.broadcast_to(padded_orders[:, None], (SLOT_PAD, LANES))
     inverse = 1.0 / lens.astype(jnp.float32)
-    smem = pl.BlockSpec(memory_space=pltpu.SMEM)
-    vmem = pl.BlockSpec(memory_space=pltpu.VMEM)
-    values, back = pl.pallas_call(
+    lane = jnp.arange(LANES)
+    lane_slot = lane % SLOT_PAD
+    lane_cycle = lane // SLOT_PAD % 2
+    padded = jnp.pad(orders, (0, spare))
+    order_lane = jnp.tile(padded, 4)
+    lens_lane = jnp.where(lane_cycle[None, :] == 1, lens[:, 1:2], lens[:, 0:1])
+    weights_lane = jnp.where(lane_cycle[None, :] == 1, weights[:, 1:2], weights[:, 0:1])
+    resolved = (2 * order_lane[None, :] < lens_lane) & (lane_slot < slot_count)[None, :]
+    double = jnp.where(order_lane == 0, 1.0, 2.0)
+    fill = ((0, CYCLE_PAD - row_total), (0, 0))
+    keep = jnp.pad(jnp.where(resolved, double[None, :], 0.0), fill)
+    factor = jnp.pad(jnp.where(resolved, weights_lane / lens_lane.astype(jnp.float32), 0.0), fill)
+    order_lane = jnp.broadcast_to(order_lane.astype(jnp.float32)[None, :], (8, LANES))
+    order_sub = jnp.broadcast_to(padded.astype(jnp.float32)[:, None], (SLOT_PAD, LANES))
+
+    line = np.arange(WAVES * 8)
+    line_slot, line_half, line_part = line // 8 * 2 + line % 8 // 4, line // 2 % 2, line % 2
+    both = np.arange(2 * LANES)
+    both_half, both_part, both_cycle, both_slot = both // LANES, both // 64 % 2, both // 32 % 2, both % 32
+    match = (
+        (line_slot[:, None] == both_slot) & (line_half[:, None] == both_half) & (line_part[:, None] == both_part)
+    )
+    spread = jnp.asarray(match, jnp.bfloat16)
+    gather = jnp.asarray(np.stack([match & (both_cycle == 0), match & (both_cycle == 1)]), jnp.bfloat16)
+
+    values, returned = pl.pallas_call(
         grid_kernel,
         out_shape=(
             jax.ShapeDtypeStruct((row_total * ROWS, LANES), jnp.bfloat16),
-            jax.ShapeDtypeStruct((row_total, 8, LANES), jnp.float32),
+            jax.ShapeDtypeStruct((WAVES, 8, LANES), jnp.bfloat16),
         ),
-        in_specs=[smem, smem, vmem, vmem, vmem],
+        in_specs=[smem, smem] + [vmem] * 7,
         out_specs=(vmem, vmem),
+        scratch_shapes=[pltpu.VMEM((2, CYCLE_PAD, LANES), jnp.float32)] * 3,
         name="cycles",
-    )(lens, inverse, order_lane, order_sub, rows)
+    )(lens, inverse, order_lane, order_sub, keep, factor, arrived, spread, gather)
     grid = values.reshape(row_total, BLOCKS, 2, LANES).transpose(2, 0, 1, 3)
     grid = grid.reshape(2, row_total, 1, LPAD)
-    returned = back[:, :2].reshape(row_total, 2, 2, 2, SLOT_PAD)[..., :slot_count].astype(jnp.bfloat16)
-    returned = returned.transpose(4, 1, 2, 0, 3).reshape(slot_count, 2, fields, 2, local_lats)
-    spectral = lax.all_to_all(returned, "wave", split_axis=0, concat_axis=4, tiled=True)
-    both = jnp.einsum("shfcq,snq->shfcn", spectral, panels, preferred_element_type=jnp.float32)
-    total = both[:, 0] + sign_flip[:, None, None, :] * both[:, 1]
+
+    blocks = pl.pallas_call(
+        back_kernel,
+        out_shape=jax.ShapeDtypeStruct((LINES, 8, width), jnp.float32),
+        in_specs=[vmem, vmem],
+        out_specs=vmem,
+        scratch_shapes=[
+            pltpu.VMEM((WAVES, 8, LANES), jnp.bfloat16),
+            pltpu.VMEM((LINES, WAVES, 8, LANES), jnp.bfloat16),
+            pltpu.VMEM((LINES, 8, width), jnp.float32),
+            dma((3,)), dma((WAVES - 1,)), dma((WAVES - 1,)),
+            dma((LINES - 1,)), dma((LINES - 1,)), dma((LINES - 1,)), dma((LINES - 1,)),
+        ],
+        compiler_params=pltpu.CompilerParams(collective_id=1, has_side_effects=True),
+        name="back",
+    )(returned, panels)
+    blocks = blocks.reshape(LINES, slots_dev, 2, 2, degrees_all // LINES, slots_dev)
+    sign_flip = jnp.where(odd, -1.0, 1.0).reshape(slots_dev, 1, LINES, degrees_all // LINES)
+    mine = jnp.stack([blocks[:, s, :, :, :, s] for s in range(slots_dev)]).transpose(0, 2, 3, 1, 4)
+    total = mine[:, 0] + sign_flip * mine[:, 1]
+    total = total.reshape(slots_dev, 1, 2, degrees_all)
     spec_out = jnp.where(retained[:, None, None, :], total, 0.0)
     return (grid, spec_out)
 

time: 191 us -> 118 us (0.62)
  waiting for transfers between devices: 114 us -> 0 us
  Pallas kernels: 16.6 us -> 88.5 us
  starting transfers between devices: 13.4 us -> 0 us
  between operations: 14.2 us -> 0.85 us
  matrix products: 8.55 us -> 0 us
  local copies, waits for them, and re-layouts: 19.1 us -> 24.4 us
    all_gather x1 -> x0, waiting for transfers between devices: 98.6 us -> none  [per_device(): panels = lax.all_gather(legendre, 'lev', axis=1, tiled=True)]
    pallas_call x0 -> x2, Pallas kernels: none -> 71.6 us  [the longest x1 48.8 us: per_device(): pl.pallas_call(front_kernel, out_shape=(jax.ShapeDtypeStruct((LEAF, depth...]
    all_to_all x2 -> x0, waiting for transfers between devices: 14.9 us -> none  [the longest x1 9.03 us: per_device(): lax.all_to_all(fourier, 'wave', split_axis=4, concat_axis=0, tiled=True)]
    all_to_all x2 -> x0, starting transfers between devices: 13.3 us -> none  [the longest x1 9.9 us: per_device(): lax.all_to_all(fourier, 'wave', split_axis=4, concat_axis=0, tiled=True)]
    dot_general x2 -> x0, matrix products: 8.55 us -> none  [the longest x1 4.69 us: per_device(): jnp.einsum('shfcq,snq->shfcn', spectral, panels, preferred_element_type=j...]
    reshape x2 -> x3, local copies, waits for them, and re-layouts: 1.6 us -> 7.16 us  [the longest x1 6.19 us: per_device(): legendre.transpose(1, 0, 2).reshape(depth * slots_dev, WAVES, row_total, 2)]
    convert_element_type x5 -> x1, local copies, waits for them, and re-layouts: 4.49 us -> 0.09 us  [per_device(): order_lane.astype(jnp.float32)[None, :]]
    unnamed x4 -> x7, local copies, waits for them, and re-layouts: 2.49 us -> 6.04 us
  transfers between devices with their start and end apart: 3 -> 0, of which waited for: 3 -> 0; matrix products, arithmetic and copies ran while one was open for 4% -> 0% of each run, Pallas kernels for 0% -> 0%
where the time goes in v2:
time: 118 us; the launch traced here: 117 us
  Pallas kernels  88.5 us (75%)
  local copies, waits for them, and re-layouts  24.4 us (21%)
  other arithmetic  3.66 us (3%)
    pallas_call x1, Pallas kernels, per_device(): pl.pallas_call(front_kernel, out_shape=(jax.ShapeDtypeStruct((LEAF, depth...  48.8 us
    pallas_call x1, Pallas kernels, per_device(): pl.pallas_call(back_kernel, out_shape=jax.ShapeDtypeStruct((LINES, 8, wid...  22.9 us
    pallas_call x1, Pallas kernels, per_device(): pl.pallas_call(grid_kernel, out_shape=(jax.ShapeDtypeStruct((row_total *...  16.9 us
    reshape x1, local copies, waits for them, and re-layouts, per_device(): legendre.transpose(1, 0, 2).reshape(depth * slots_dev, WAVES, row_total, 2)  6.19 us
    unnamed x7, local copies, waits for them, and re-layouts  6.04 us

profile of v2, /device:TPU:1, one launch (start us, length us, event | category | flops | bytes accessed | tf_op | source)
XLA Modules:
  0.0 117.4 jit_solution(4753806839094787093)
XLA Ops:
  0.6 0.7 and_select_fusion.5
  1.5 0.7 broadcast_select_fusion.1
  2.4 0.2 copy.50
  2.7 0.4 broadcast_in_dim.194
  3.1 0.3 copy.51
  3.4 0.4 broadcast_in_dim.187
  3.8 0.6 broadcast_select_fusion.coef_ref
  4.5 6.2 %reshape.237 = bf16[40,12,50,2]{3,2,1,0:T(8,128)(2,1)} reshape(bf16[20,2,1200]{2,1,0:T(2,128)(2,1)S(1)} %bitcast.36) | data formatting | bytes 192000 | tf_op jit(solution)/shard_map/reshape | solution.py:314
  10.6 6.0 %copy.58 = bf16[40,12,2,50]{3,2,1,0:T(2,128)(2,1)S(1)} copy(bf16[40,12,2,50]{2,3,1,0:T(8,128)(2,1)} %bitcast.27) | data formatting | bytes 192000
  16.7 0.3 pad.19.clone
  16.9 0.9 reshape.238.leg_ref
  17.8 48.8 %front.1 = (bf16[8,40,1536]{2,1,0:T(8,128)(2,1)}, bf16[12,8,128]{2,1,0:T(8,128)(2,1)}) custom-call(bf16[40,1536]{1,0:T(8,128)(2,1)} %reshape.238.leg_ref, bf16[8,8,320]{2,1,0:T(8,128)(2,1)} %broadcast_select_fusion.coef_ref), custom_call_target="tpu_custom_call" | custom-call | tf_op jit(solution)/shard_map/front/pallas_call | solution.py:330
  66.6 0.8 dynamic_slice.9
  67.4 0.1 reshape.235.len_ref
  67.5 0.2 slice_reduce_fusion.3
  67.7 0.8 dynamic_slice.10
  68.4 0.1 reshape.236
  68.6 0.2 slice_reduce_fusion.1
  69.1 0.6 pad.17.keep_ref
  69.7 0.6 pad.18.factor_ref
  70.3 0.6 convert_divide_fusion.inv_ref
  70.9 0.7 broadcast_in_dim.172.order_sub_ref
  71.7 0.6 broadcast_in_dim.171.order_lane_ref
  72.3 16.9 %cycles.1 = (bf16[3800,128]{1,0:T(8,128)(2,1)}, bf16[12,8,128]{2,1,0:T(8,128)(2,1)}) custom-call(s32[50,2]{1,0:T(8,128)} %copy-done.1, f32[50,2]{1,0:T(8,128)} %convert_divide_fusion.inv_ref, f32[8,128]{1,0:T(8,128)} %broadcast_in_dim.171.order_lane_ref, f32[32,128]{1,0:T(8,128)} %broadcast_in_dim.172.order_sub_ref, f32[64,128]{1,0:T(8,128)} %pad.17.keep_ref, ...), custom_call_target="tpu_custom_call" | custom-call | tf_op jit(solution)/shard_map/cycles/pallas_call | solution.py:380
  89.1 22.9 %back.1 = f32[8,8,320]{2,1,0:T(8,128)} custom-call(bf16[12,8,128]{2,1,0:T(8,128)(2,1)} %get-tuple-element.8.ret_ref, bf16[8,40,1536]{2,1,0:T(8,128)(2,1)} %get-tuple-element.9.panel_ref), custom_call_target="tpu_custom_call" | custom-call | tf_op jit(solution)/shard_map/back/pallas_call | solution.py:394
  112.0 1.3 %copy.53 = f32[8,8,320]{0,2,1:T(8,128)S(1)} copy(f32[8,8,320]{2,1,0:T(8,128)} %back.1) | data formatting | bytes 163840 | tf_op jit(solution)/shard_map/back/pallas_call | solution.py:394
  113.3 0.6 fusion.10
  113.9 0.2 copy.54
  114.1 0.2 copy.55
  114.7 0.6 select_bitcast_fusion
  115.3 0.1 copy.60
  115.5 2.0 %reshape.240 = bf16[2,50,1,4864]{3,0,1,2:T(2,128)(2,1)} reshape(bf16[2,50,38,128]{3,2,0,1:T(8,128)(2,1)S(1)} %bitcast.28) | data formatting | bytes 1945600 | tf_op jit(solution)/shard_map/reshape | solution.py:392
  (30 shorter events, 1.2 us)
Async XLA Ops:
  2.2 2.2 %copy-start.2 = (bf16[2,20,1200]{2,0,1:T(2,128)(2,1)S(1)}, bf16[2,20,1200]{2,0,1:T(2,128)(2,1)}, u32[]{:S(2)}) copy-start(bf16[2,20,1200]{2,0,1:T(2,128)(2,1)} %param.8) | copy-start | bytes 288004
  67.5 4.8 %copy-start.1 = (s32[50,2]{1,0:T(8,128)}, s32[50,2]{1,0:T(8,128)S(1)}, u32[]{:S(2)}) copy-start(s32[50,2]{1,0:T(8,128)S(1)} %reshape.235.len_ref) | copy-start | bytes 1204
  113.3 2.0 %copy-start = (bf16[3800,128]{1,0:T(8,128)(2,1)S(1)}, bf16[3800,128]{1,0:T(8,128)(2,1)}, u32[]{:S(2)}) copy-start(bf16[3800,128]{1,0:T(8,128)(2,1)} %get-tuple-element.7) | copy-start | bytes 2918404

commit v3 on v2

--- a/solution.py
+++ b/solution.py
@@ -18,7 +18,11 @@
 WAVES = 12
 LINES = 8
 LEAF = 8
-LATS = WAVES * LANES
+LATS = 1200
+OWN = LATS // WAVES
+DEGREES = 1280
+SPAN = DEGREES // LINES
+SLOTS = 24
 MESH = pl.DeviceIdType.MESH
 NT = (((1,), (1,)), ((), ()))
 
@@ -63,6 +67,10 @@
     )
 
 
+def order_of(map_ref, wave, slot):
+    return map_ref[wave * 2 + slot] * DEGREES // SLOTS
+
+
 def greet(devices):
     barrier = pltpu.get_barrier_semaphore()
     for device in devices:
@@ -71,7 +79,7 @@
 
 
 def front_kernel(
-    leg_ref, coef_ref, panel_ref, waves_ref, lhs, part, got, four,
+    map_ref, leg_ref, spec_ref, panel_ref, waves_ref, lhs, part, got, four,
     local_sem, chip_send, chip_recv, core_send, core_recv, coef_send, coef_recv,
     part_send, part_recv, wave_send, wave_recv,
 ):
@@ -90,8 +98,7 @@
         copy.start()
         copies.append(copy)
     for d in range(1, LINES):
-        target = lax.rem(line + d, LINES)
-        copy = remote(coef_ref.at[target], lhs.at[line], coef_send.at[d - 1], coef_recv.at[d - 1], lines[d - 1])
+        copy = remote(spec_ref, lhs.at[line], coef_send.at[d - 1], coef_recv.at[d - 1], lines[d - 1])
         copy.start()
         copies.append(copy)
     copy = remote(leg_ref, panel_ref.at[leaf], core_send.at[0], core_recv.at[0], sibling)
@@ -99,8 +106,25 @@
     copies.append(copy)
     own_panel = pltpu.make_async_copy(leg_ref, panel_ref.at[leaf], local_sem.at[0])
     own_panel.start()
-    own_coef = pltpu.make_async_copy(coef_ref.at[line], lhs.at[line], local_sem.at[1])
+    own_coef = pltpu.make_async_copy(spec_ref, lhs.at[line], local_sem.at[1])
     own_coef.start()
+    width = panel_ref.shape[0] * panel_ref.shape[1]
+    picked = lax.broadcasted_iota(jnp.int32, (DEGREES, width), 0) - line * SPAN
+    widen = jnp.where(picked == lax.broadcasted_iota(jnp.int32, (DEGREES, width), 1) // 2, 1.0, 0.0)
+    widen = widen.astype(jnp.bfloat16)
+    four[...] = jnp.zeros_like(four)
+    own_coef.wait()
+    for d in range(1, LINES):
+        block = lhs.at[lax.rem(line + LINES - d, LINES)]
+        remote(block, block, coef_send.at[d - 1], coef_recv.at[d - 1], lines[d - 1]).wait_recv()
+    coef = jnp.dot(lhs[...].reshape(LINES * 8, DEGREES), widen, preferred_element_type=jnp.float32)
+    kind = lax.broadcasted_iota(jnp.int32, coef.shape, 0) % 8
+    column = lax.broadcasted_iota(jnp.int32, coef.shape, 1)
+    degree = column // 2 + line * SPAN
+    order = jnp.where(kind >= 4, order_of(map_ref, wave, 1), order_of(map_ref, wave, 0))
+    coef = jnp.where((kind // 4 == column % 2) & (degree >= order), coef, 0.0)
+    coef = jnp.where((kind // 2 % 2 == 1) & ((degree + order) % 2 == 1), -coef, coef)
+    coef = coef.astype(jnp.bfloat16)
     for d in range(1, 4):
         origin = lax.rem(chip + 4 - d, 4) * 2 + core
         block = panel_ref.at[origin]
@@ -109,20 +133,11 @@
         copy.start()
         copies.append(copy)
     own_panel.wait()
-    own_coef.wait()
     for d in range(4):
         origin = lax.rem(chip + 4 - d, 4) * 2 + 1 - core
         block = panel_ref.at[origin]
         remote(block, block, core_send.at[d], core_recv.at[d], sibling).wait_recv()
-    for d in range(1, LINES):
-        block = lhs.at[lax.rem(line + LINES - d, LINES)]
-        remote(block, block, coef_send.at[d - 1], coef_recv.at[d - 1], lines[d - 1]).wait_recv()
-
-    depth = panel_ref.shape[1]
-    panel = panel_ref[...].reshape(LEAF * depth, LATS)
-    product = jnp.dot(
-        lhs[...].reshape(LINES * 8, LEAF * depth), panel, preferred_element_type=jnp.float32
-    )
+    product = jnp.dot(coef, panel_ref[...].reshape(width, LATS), preferred_element_type=jnp.float32)
     part[...] = product.reshape(LINES, 8, LATS)
     for d in range(1, LINES):
         target = lax.rem(line + d, LINES)
@@ -135,7 +150,7 @@
         remote(block, block, part_send.at[d - 1], part_recv.at[d - 1], lines[d - 1]).wait_recv()
         total = total + got[d - 1]
     for w in range(WAVES):
-        four[w] = total[:, w * LANES : (w + 1) * LANES].astype(jnp.bfloat16)
+        four[w, :, :OWN] = total[:, w * OWN : (w + 1) * OWN].astype(jnp.bfloat16)
     for d in range(1, WAVES):
         target = lax.rem(wave + d, WAVES)
         copy = remote(four.at[target], waves_ref.at[wave], wave_send.at[d - 1], wave_recv.at[d - 1], waves[d - 1])
@@ -152,7 +167,7 @@
 
 
 def back_kernel(
-    ret_ref, panel_ref, out_ref, here, fields, part,
+    map_ref, ret_ref, panel_ref, out_ref, here, fields, part, final,
     local_sem, wave_send, wave_recv, line_send, line_recv, part_send, part_recv,
 ):
     wave, lev, line, leaf = where_am_i()
@@ -183,28 +198,52 @@
         remote(block, block, line_send.at[d - 1], line_recv.at[d - 1], lines[d - 1]).wait_recv()
     depth = panel_ref.shape[1]
     panel = panel_ref[...].reshape(LEAF * depth, LATS)
-    lhs = jnp.concatenate([fields[:, w].reshape(LINES * 8, LANES) for w in range(WAVES)], 1)
+    lhs = jnp.concatenate(
+        [fields[:, w].reshape(LINES * 8, LANES)[:, :OWN].astype(jnp.float32) for w in range(WAVES)], 1
+    ).astype(jnp.bfloat16)
     product = lax.dot_general(lhs, panel, NT, preferred_element_type=jnp.float32)
-    part[...] = product.reshape(LINES, 8, LEAF * depth)
+    width = LEAF * depth
+    kind = lax.broadcasted_iota(jnp.int32, product.shape, 0) % 8
+    column = lax.broadcasted_iota(jnp.int32, product.shape, 1)
+    order = jnp.where(kind >= 4, order_of(map_ref, wave, 1), order_of(map_ref, wave, 0))
+    degree = column // 2 + line * SPAN
+    product = jnp.where((kind // 4 == column % 2) & (degree >= order), product, 0.0)
+    product = jnp.where((kind // 2 % 2 == 1) & ((degree + order) % 2 == 1), -product, product)
+    narrow = lax.broadcasted_iota(jnp.int32, (width, SPAN), 0) // 2 == lax.broadcasted_iota(jnp.int32, (width, SPAN), 1)
+    narrow = jnp.where(narrow, 1.0, 0.0)
+    product = jnp.dot(
+        product, narrow, precision=lax.Precision.HIGHEST, preferred_element_type=jnp.float32
+    ).reshape(LINES, 8, SPAN)
+    part[...] = product
     for d in range(1, LINES):
         target = lax.rem(line + d, LINES)
-        copy = remote(part.at[target], out_ref.at[line], part_send.at[d - 1], part_recv.at[d - 1], lines[d - 1])
-        copy.start()
-        copies.append(copy)
-    own_part = pltpu.make_async_copy(part.at[line], out_ref.at[line], local_sem.at[2])
+        copy = remote(part.at[target], final.at[line], part_send.at[d - 1], part_recv.at[d - 1], lines[d - 1])
+        copy.start()
+        copies.append(copy)
+    own_part = pltpu.make_async_copy(part.at[line], final.at[line], local_sem.at[2])
     own_part.start()
     own_part.wait()
     for d in range(1, LINES):
-        block = out_ref.at[lax.rem(line + LINES - d, LINES)]
+        block = final.at[lax.rem(line + LINES - d, LINES)]
         remote(block, block, part_send.at[d - 1], part_recv.at[d - 1], lines[d - 1]).wait_recv()
+    total = jnp.concatenate([final[y] for y in range(LINES)], 1)
+    for s in range(2):
+        out_ref[s] = total[4 * s : 4 * s + 2] + total[4 * s + 2 : 4 * s + 4]
     for copy in copies:
         copy.wait_send()
 
 
 def grid_kernel(
-    len_ref, inv_ref, order_lane_ref, order_sub_ref, keep_ref, factor_ref, wave_ref, spread_ref, gather_ref,
-    grid_ref, ret_ref, plain_ref, cross_ref, sum_ref,
+    len_ref, weight_ref, order_ref, wave_ref, spread_ref, gather_ref, natural_ref,
+    grid_ref, ret_ref, turned_ref, plain_ref, cross_ref, sum_ref,
 ):
+    first_lat = lax.axis_index("wave") * OWN
+    order_lane = order_ref[0:1, :]
+    order_lane = order_lane + pltpu.roll(order_lane, 32, 1)
+    order_lane = order_lane + pltpu.roll(order_lane, 64, 1)
+    lane_slot = lax.broadcasted_iota(jnp.int32, (1, LANES), 1) % SLOT_PAD
+    double = jnp.where(lane_slot < SLOTS, jnp.where(order_lane == 0.0, 1.0, 2.0), 0.0)
+    order_sub = jnp.broadcast_to(order_lane, (LANES, LANES)).T[:SLOT_PAD]
     lane_f = lax.broadcasted_iota(jnp.int32, (ROWS_PAD, LANES), 1)
     row_f = lax.broadcasted_iota(jnp.int32, (ROWS_PAD, LANES), 0)
     block_start = (row_f // 2) * LANES
@@ -212,32 +251,39 @@
     block_start = block_start.astype(jnp.float32)
     second_lane = (lax.broadcasted_iota(jnp.int32, (1, LANES), 1) // SLOT_PAD) % 2 == 1
     sign = jnp.where(lax.broadcasted_iota(jnp.int32, (1, LANES), 1) < 64, 1.0, -1.0)
-    order_lane = order_lane_ref[0:1, :]
     inner_lane = lax.broadcasted_iota(jnp.int32, (SLOT_PAD, LANES), 1).astype(jnp.float32)
-    inner_product = order_sub_ref[...] * inner_lane
+    inner_product = order_sub * inner_lane
     north = (lax.broadcasted_iota(jnp.int32, (ROWS_PAD, LANES), 0) % 2) == 0
     arrived = wave_ref[...].reshape(WAVES * 8, LANES)
     turned = lax.dot_general(
         arrived, spread_ref[...], (((0,), (0,)), ((), ())), preferred_element_type=jnp.float32
     )
     for h in range(2):
-        part = turned[:, h * LANES : (h + 1) * LANES]
-        part = jnp.where(second_lane, part[CYCLE_PAD:], part[:CYCLE_PAD]) * keep_ref[...]
+        turned_ref[...] = turned[:, h * LANES : (h + 1) * LANES]
+        part = jnp.where(
+            second_lane, turned_ref[pl.ds(1, CYCLE_PAD, 2), :], turned_ref[pl.ds(0, CYCLE_PAD, 2), :]
+        )
+        part = part * double
         plain_ref[h] = part
         cross_ref[h] = -sign * pltpu.roll(part, 64, 1)
     sum_ref[...] = jnp.zeros_like(sum_ref)
     zero_block = jnp.zeros((SLOT_PAD, LANES), jnp.bfloat16)
 
     def one_row(row):
-        first = len_ref[row, 0]
-        second = len_ref[row, 1]
+        first = len_ref[first_lat + 2 * row]
+        second = len_ref[first_lat + 2 * row + 1]
         first_f = first.astype(jnp.float32)
         second_f = second.astype(jnp.float32)
-        inv_first = inv_ref[row, 0]
-        inv_second = inv_ref[row, 1]
         length_lane = jnp.where(second_lane, second_f, first_f)
-        inverse_lane = jnp.where(second_lane, inv_second, inv_first)
         start_lane = jnp.where(second_lane, first_f, 0.0)
+        inverse_lane = 1.0 / length_lane
+        inv_first = inverse_lane[:, 0:1]
+        inv_second = inverse_lane[:, SLOT_PAD : SLOT_PAD + 1]
+        weight_lane = jnp.where(
+            second_lane, weight_ref[first_lat + 2 * row + 1], weight_ref[first_lat + 2 * row]
+        )
+        resolved = 2.0 * order_lane < length_lane
+        factor = jnp.where(resolved, weight_lane * inverse_lane, 0.0)
         outer = order_lane * (block_start - start_lane)
         outer_cos, outer_sin = cos_sin_turns(turns_of(outer, length_lane, inverse_lane))
         cos_a, sin_a = cos_sin_turns(turns_of(inner_product, first_f, inv_first))
@@ -253,7 +299,7 @@
         )
         plain = jnp.where(north, plain_ref[0, pl.ds(row, 1), :], plain_ref[1, pl.ds(row, 1), :])
         crossed = jnp.where(north, cross_ref[0, pl.ds(row, 1), :], cross_ref[1, pl.ds(row, 1), :])
-        spread = (plain * outer_cos + crossed * outer_sin).astype(jnp.bfloat16)
+        spread = jnp.where(resolved, plain * outer_cos + crossed * outer_sin, 0.0).astype(jnp.bfloat16)
         images = lax.dot_general(
             spread, inner, (((1,), (0,)), ((), ())), preferred_element_type=jnp.float32
         )
@@ -278,18 +324,18 @@
         total = cos_sum + sign * pltpu.roll(sin_sum, 64, 1)
         total = total + pltpu.roll(total, 4, 0)
         total = total + pltpu.roll(total, 2, 0)
-        sum_ref[0, pl.ds(row, 1), :] = total[0:1, :]
-        sum_ref[1, pl.ds(row, 1), :] = total[1:2, :]
+        sum_ref[0, pl.ds(row, 1), :] = total[0:1, :] * factor
+        sum_ref[1, pl.ds(row, 1), :] = total[1:2, :] * factor
         return values
 
-    @pl.loop(0, len_ref.shape[0] // 2)
+    @pl.loop(0, OWN // 4)
     def _(pair):
         even = one_row(2 * pair)
         odd = one_row(2 * pair + 1)
         start = pl.multiple_of(pair * 2 * ROWS, 8)
         grid_ref[pl.ds(start, 2 * ROWS), :] = jnp.concatenate([even[:ROWS], odd[:ROWS]], 0)
 
-    sums = jnp.concatenate([sum_ref[0] * factor_ref[...], sum_ref[1] * factor_ref[...]], 1).astype(jnp.bfloat16)
+    sums = jnp.concatenate([sum_ref[0], sum_ref[1]], 1).astype(jnp.bfloat16)
     returned = jnp.concatenate(
         [
             lax.dot_general(gather_ref[cycle], sums, NT, preferred_element_type=jnp.float32)
@@ -297,31 +343,17 @@
         ],
         1,
     )
+    returned = jnp.dot(returned.astype(jnp.bfloat16), natural_ref[...], preferred_element_type=jnp.float32)
     ret_ref[...] = returned.astype(jnp.bfloat16).reshape(WAVES, 8, LANES)
 
 def per_device(spec, legendre, gauss_w, cycle_len, wave_map):
-    slots_dev, _, _, degrees_all = spec.shape
+    slots_dev = spec.shape[0]
     depth = legendre.shape[1]
-    slot_count = wave_map.shape[0]
-    orders = wave_map * degrees_all // slot_count
-    wave_pos = lax.axis_index("wave")
-    own_orders = lax.dynamic_slice_in_dim(orders, wave_pos * slots_dev, slots_dev)
-    degrees = jnp.arange(degrees_all, dtype=jnp.int32)
-    local_lats = cycle_len.shape[0] // WAVES
-    row_total = local_lats // 2
-    spare = SLOT_PAD - slot_count
-
-    panel = legendre.transpose(1, 0, 2).reshape(depth * slots_dev, WAVES, row_total, 2).transpose(0, 1, 3, 2)
-    panel = jnp.pad(panel, ((0, 0), (0, 0), (0, 0), (0, CYCLE_PAD - row_total))).reshape(depth * slots_dev, LATS)
-
-    retained = degrees[None, :] >= own_orders[:, None]
-    odd = (degrees[None, :] + own_orders[:, None]) % 2 == 1
-    coefficients = jnp.where(retained[:, None, :], spec[:, 0], jnp.zeros((), jnp.bfloat16))
-    flipped = jnp.where(odd[:, None, :], -coefficients, coefficients)
-    stacked = jnp.stack([coefficients, flipped], 1).reshape(slots_dev, 4, LINES, degrees_all // LINES, 1)
-    same = jnp.arange(slots_dev)[:, None, None, None, None] == jnp.arange(slots_dev)
-    coef = jnp.where(same, stacked, jnp.zeros((), jnp.bfloat16)).transpose(2, 0, 1, 3, 4)
-    coef = coef.reshape(LINES, 8, degrees_all // LINES * slots_dev)
+    row_total = OWN // 2
+    panel = legendre.transpose(1, 0, 2).reshape(depth * slots_dev, LATS)
+    doubled = jnp.broadcast_to(spec, (slots_dev, 2, 2, DEGREES)).reshape(8, DEGREES)
+    orders = (wave_map * DEGREES // SLOTS).astype(jnp.float32)
+    orders = jnp.broadcast_to(jnp.pad(orders, (0, LANES - SLOTS))[None, :], (8, LANES))
 
     vmem = pl.BlockSpec(memory_space=pltpu.VMEM)
     smem = pl.BlockSpec(memory_space=pltpu.SMEM)
@@ -333,10 +365,10 @@
             jax.ShapeDtypeStruct((LEAF, depth * slots_dev, LATS), jnp.bfloat16),
             jax.ShapeDtypeStruct((WAVES, 8, LANES), jnp.bfloat16),
         ),
-        in_specs=[vmem, vmem],
+        in_specs=[smem, vmem, vmem],
         out_specs=(vmem, vmem),
         scratch_shapes=[
-            pltpu.VMEM((LINES, 8, width), jnp.bfloat16),
+            pltpu.VMEM((LINES, 8, DEGREES), jnp.bfloat16),
             pltpu.VMEM((LINES, 8, LATS), jnp.float32),
             pltpu.VMEM((LINES - 1, 8, LATS), jnp.float32),
             pltpu.VMEM((WAVES, 8, LANES), jnp.bfloat16),
@@ -346,26 +378,7 @@
         ],
         compiler_params=pltpu.CompilerParams(collective_id=0, has_side_effects=True),
         name="front",
-    )(panel, coef)
-
-    lat_start = wave_pos * local_lats
-    lens = lax.dynamic_slice_in_dim(cycle_len, lat_start, local_lats).reshape(row_total, 2)
-    weights = lax.dynamic_slice_in_dim(gauss_w, lat_start, local_lats).reshape(row_total, 2)
-    inverse = 1.0 / lens.astype(jnp.float32)
-    lane = jnp.arange(LANES)
-    lane_slot = lane % SLOT_PAD
-    lane_cycle = lane // SLOT_PAD % 2
-    padded = jnp.pad(orders, (0, spare))
-    order_lane = jnp.tile(padded, 4)
-    lens_lane = jnp.where(lane_cycle[None, :] == 1, lens[:, 1:2], lens[:, 0:1])
-    weights_lane = jnp.where(lane_cycle[None, :] == 1, weights[:, 1:2], weights[:, 0:1])
-    resolved = (2 * order_lane[None, :] < lens_lane) & (lane_slot < slot_count)[None, :]
-    double = jnp.where(order_lane == 0, 1.0, 2.0)
-    fill = ((0, CYCLE_PAD - row_total), (0, 0))
-    keep = jnp.pad(jnp.where(resolved, double[None, :], 0.0), fill)
-    factor = jnp.pad(jnp.where(resolved, weights_lane / lens_lane.astype(jnp.float32), 0.0), fill)
-    order_lane = jnp.broadcast_to(order_lane.astype(jnp.float32)[None, :], (8, LANES))
-    order_sub = jnp.broadcast_to(padded.astype(jnp.float32)[:, None], (SLOT_PAD, LANES))
+    )(wave_map, panel, doubled)
 
     line = np.arange(WAVES * 8)
     line_slot, line_half, line_part = line // 8 * 2 + line % 8 // 4, line // 2 % 2, line % 2
@@ -375,6 +388,11 @@
         (line_slot[:, None] == both_slot) & (line_half[:, None] == both_half) & (line_part[:, None] == both_part)
     )
     spread = jnp.asarray(match, jnp.bfloat16)
+    packed = np.arange(LANES)
+    natural = (packed % CYCLE_PAD < row_total)[:, None] & (
+        (packed % CYCLE_PAD * 2 + packed // CYCLE_PAD)[:, None] == packed[None, :]
+    )
+    natural = jnp.asarray(natural, jnp.bfloat16)
     gather = jnp.asarray(np.stack([match & (both_cycle == 0), match & (both_cycle == 1)]), jnp.bfloat16)
 
     values, returned = pl.pallas_call(
@@ -383,35 +401,31 @@
             jax.ShapeDtypeStruct((row_total * ROWS, LANES), jnp.bfloat16),
             jax.ShapeDtypeStruct((WAVES, 8, LANES), jnp.bfloat16),
         ),
-        in_specs=[smem, smem] + [vmem] * 7,
+        in_specs=[smem, smem] + [vmem] * 5,
         out_specs=(vmem, vmem),
-        scratch_shapes=[pltpu.VMEM((2, CYCLE_PAD, LANES), jnp.float32)] * 3,
+        scratch_shapes=[pltpu.VMEM((LANES, LANES), jnp.float32)] + [pltpu.VMEM((2, CYCLE_PAD, LANES), jnp.float32)] * 3,
         name="cycles",
-    )(lens, inverse, order_lane, order_sub, keep, factor, arrived, spread, gather)
+    )(cycle_len, gauss_w, orders, arrived, spread, gather, natural)
     grid = values.reshape(row_total, BLOCKS, 2, LANES).transpose(2, 0, 1, 3)
     grid = grid.reshape(2, row_total, 1, LPAD)
 
-    blocks = pl.pallas_call(
+    spec_out = pl.pallas_call(
         back_kernel,
-        out_shape=jax.ShapeDtypeStruct((LINES, 8, width), jnp.float32),
-        in_specs=[vmem, vmem],
+        out_shape=jax.ShapeDtypeStruct((slots_dev, 2, DEGREES), jnp.float32),
+        in_specs=[smem, vmem, vmem],
         out_specs=vmem,
         scratch_shapes=[
             pltpu.VMEM((WAVES, 8, LANES), jnp.bfloat16),
             pltpu.VMEM((LINES, WAVES, 8, LANES), jnp.bfloat16),
-            pltpu.VMEM((LINES, 8, width), jnp.float32),
+            pltpu.VMEM((LINES, 8, SPAN), jnp.float32),
+            pltpu.VMEM((LINES, 8, SPAN), jnp.float32),
             dma((3,)), dma((WAVES - 1,)), dma((WAVES - 1,)),
             dma((LINES - 1,)), dma((LINES - 1,)), dma((LINES - 1,)), dma((LINES - 1,)),
         ],
         compiler_params=pltpu.CompilerParams(collective_id=1, has_side_effects=True),
         name="back",
-    )(returned, panels)
-    blocks = blocks.reshape(LINES, slots_dev, 2, 2, degrees_all // LINES, slots_dev)
-    sign_flip = jnp.where(odd, -1.0, 1.0).reshape(slots_dev, 1, LINES, degrees_all // LINES)
-    mine = jnp.stack([blocks[:, s, :, :, :, s] for s in range(slots_dev)]).transpose(0, 2, 3, 1, 4)
-    total = mine[:, 0] + sign_flip * mine[:, 1]
-    total = total.reshape(slots_dev, 1, 2, degrees_all)
-    spec_out = jnp.where(retained[:, None, None, :], total, 0.0)
+    )(wave_map, returned, panels)
+    spec_out = spec_out.reshape(slots_dev, 1, 2, DEGREES)
     return (grid, spec_out)
 
 

time: 118 us -> 96.6 us (0.82)
  local copies, waits for them, and re-layouts: 24.4 us -> 6.77 us
  other arithmetic: 3.66 us -> 0.67 us
    unnamed x7 -> x5, local copies, waits for them, and re-layouts: 6.04 us -> 0.61 us
    reshape x4 -> x2, local copies, waits for them, and re-layouts: 7.27 us -> 2.22 us  [the longest x1 1.6 us: per_device(): panel = legendre.transpose(1, 0, 2).reshape(depth * slots_dev, LATS)]
    pallas_call x1, Pallas kernels: 48.8 us -> 46.5 us  [per_device(): pl.pallas_call(front_kernel, out_shape=(jax.ShapeDtypeStruct((LEAF, depth...]
    select_n x6 -> x0, other arithmetic: 2.24 us -> none  [the longest x1 0.75 us: per_device(): flipped = jnp.where(odd[:, None, :], -coefficients, coefficients)]
    broadcast_in_dim x8 -> x2, local copies, waits for them, and re-layouts: 2.73 us -> 0.61 us  [the longest x1 0.59 us: per_device(): jnp.broadcast_to(jnp.pad(orders, (0, LANES - SLOTS))[None, :], (8, LANES))]
    dynamic_slice x3 -> x0, local copies, waits for them, and re-layouts: 1.64 us -> none  [the longest x1 0.78 us: per_device(): lax.dynamic_slice_in_dim(gauss_w, lat_start, local_lats)]
    pad x3 -> x1, local copies, waits for them, and re-layouts: 1.49 us -> 0.01 us  [per_device(): jnp.pad(orders, (0, LANES - SLOTS))[None, :]]
    pallas_call x1 -> x0, local copies, waits for them, and re-layouts: 1.31 us -> none  [per_device(): pl.pallas_call(back_kernel, out_shape=jax.ShapeDtypeStruct((LINES, 8, wid...]
where the time goes in v3:
time: 96.6 us; the launch traced here: 96.3 us
  Pallas kernels  88.1 us (91%)
  local copies, waits for them, and re-layouts  6.77 us (7%)
    pallas_call x1, Pallas kernels, per_device(): pl.pallas_call(front_kernel, out_shape=(jax.ShapeDtypeStruct((LEAF, depth...  46.5 us
    pallas_call x1, Pallas kernels, per_device(): pl.pallas_call(back_kernel, out_shape=jax.ShapeDtypeStruct((slots_dev, 2,...  23.6 us
    pallas_call x1, Pallas kernels, per_device(): pl.pallas_call(grid_kernel, out_shape=(jax.ShapeDtypeStruct((row_total *...  18 us
    reshape x1, local copies, waits for them, and re-layouts, per_device(): grid = grid.reshape(2, row_total, 1, LPAD)  1.98 us

profile of v3, /device:TPU:1, one launch (start us, length us, event | category | flops | bytes accessed | tf_op | source)
XLA Modules:
  0.0 96.3 jit_solution(5347794940997074250)
XLA Ops:
  0.6 0.0 copy-start.1
  0.6 0.7 fusion
  1.3 0.6 broadcast_in_dim.6.order_ref
  1.9 0.0 copy-done.1
  1.9 0.6 reshape.21.spec_ref
  2.6 1.6 %reshape.20.leg_ref = bf16[40,1200]{1,0:T(8,128)(2,1)} reshape(bf16[20,2,1200]{2,1,0:T(2,128)(2,1)} %bitcast.15) | data formatting | bytes 192000 | tf_op jit(solution)/shard_map/reshape | solution.py:353
  4.2 46.5 %front.1 = (bf16[8,40,1200]{2,1,0:T(8,128)(2,1)}, bf16[12,8,128]{2,1,0:T(8,128)(2,1)}) custom-call(s32[24]{0:T(128)} %map_ref.3, bf16[40,1200]{1,0:T(8,128)(2,1)} %reshape.20.leg_ref, bf16[8,1280]{1,0:T(8,128)(2,1)} %reshape.21.spec_ref), custom_call_target="tpu_custom_call" | custom-call | tf_op jit(solution)/shard_map/front/pallas_call | solution.py:362
  50.7 18.0 %cycles.1 = (bf16[3800,128]{1,0:T(8,128)(2,1)}, bf16[12,8,128]{2,1,0:T(8,128)(2,1)}) custom-call(s32[1200]{0:T(1024)} %len_ref.1, f32[1200]{0:T(1024)} %weight_ref.1, f32[8,128]{1,0:T(8,128)} %broadcast_in_dim.6.order_ref, bf16[12,8,128]{2,1,0:T(8,128)(2,1)} %get-tuple-element.6.wave_ref, bf16[96,256]{1,0:T(8,128)(2,1)} %constant.22.clone.spread_ref, ...), custom_call_target="tpu_custom_call" | custom-call | tf_op jit(solution)/shard_map/cycles/pallas_call | solution.py:398
  68.7 23.6 %back.1 = f32[2,2,1280]{2,1,0:T(2,128)} custom-call(s32[24]{0:T(128)} %map_ref.3, bf16[12,8,128]{2,1,0:T(8,128)(2,1)} %get-tuple-element.8.ret_ref, bf16[8,40,1200]{2,1,0:T(8,128)(2,1)} %get-tuple-element.9.panel_ref), custom_call_target="tpu_custom_call" | custom-call | tf_op jit(solution)/shard_map/back/pallas_call | solution.py:412
  92.3 1.3 %copy.16 = bf16[50,38,2,128]{3,1,2,0:T(8,128)(2,1)S(1)} copy(bf16[50,38,2,128]{3,2,1,0:T(2,128)(2,1)} %bitcast.13) | data formatting | bytes 1945600 | tf_op jit(solution)/shard_map/reshape | solution.py:409
  93.7 0.0 copy-start
  93.7 2.0 %reshape.23 = bf16[2,50,1,4864]{3,0,1,2:T(2,128)(2,1)} reshape(bf16[2,50,38,128]{3,2,0,1:T(8,128)(2,1)S(1)} %bitcast.12) | data formatting | bytes 1945600 | tf_op jit(solution)/shard_map/reshape | solution.py:410
  95.7 0.0 copy-done
  95.7 0.6 copy.18
  (2 shorter events, 0.0 us)
Async XLA Ops:
  0.6 1.3 %copy-start.1 = (bf16[2,1,2,1280]{3,2,1,0:T(2,128)(2,1)S(1)}, bf16[2,1,2,1280]{3,2,1,0:T(2,128)(2,1)}, u32[]{:S(2)}) copy-start(bf16[2,1,2,1280]{3,2,1,0:T(2,128)(2,1)} %param.8) | copy-start | bytes 30724
  93.7 2.0 %copy-start = (f32[2,2,1280]{2,1,0:T(2,128)S(1)}, f32[2,2,1280]{2,1,0:T(2,128)}, u32[]{:S(2)}) copy-start(f32[2,2,1280]{2,1,0:T(2,128)} %back.1) | copy-start | bytes 61444

commit v4 on v1

v4 whole, which is shorter than its diff:
```python
import math

import jax
import jax.numpy as jnp
import numpy as np
from jax import lax
from jax.experimental import pallas as pl
from jax.experimental.pallas import tpu as pltpu
from jax.sharding import PartitionSpec as P

LPAD = 4864
LANES = 128
BLOCKS = LPAD // LANES
ROWS_PAD = 80
SLOT_PAD = 32
CYCLE_PAD = 64
WAVES = 12
LINES = 8
LEAF = 8
LATS = 1200
OWN = LATS // WAVES
GRID_ROWS = OWN // 2
DEGREES = 1280
SPAN = DEGREES // LINES
SLOTS = 24
EARLY_ROWS = 20
MESH = pl.DeviceIdType.MESH
NT = (((1,), (1,)), ((), ()))


def cos_sin_turns(turns):
    quarter = turns * 4.0
    whole = jnp.round(quarter)
    rest = (quarter - whole) * (0.5 * math.pi)
    square = rest * rest
    sine = rest + rest * square * (
        -1.6666666666e-1 + square * (8.3333331e-3 + square * (-1.98412698e-4 + square * 2.7557319e-6))
    )
    cosine = 1.0 + square * (
        -0.5 + square * (4.16666667e-2 + square * (-1.388888889e-3 + square * (2.48015873e-5 - square * 2.7557319e-7)))
    )
    step = whole.astype(jnp.int32) & 3
    swap = (step & 1) == 1
    cos_base = jnp.where(swap, sine, cosine)
    sin_base = jnp.where(swap, cosine, sine)
    cos_value = jnp.where((step == 1) | (step == 2), -cos_base, cos_base)
    sin_value = jnp.where(step >= 2, -sin_base, sin_base)
    return cos_value, sin_value


def turns_of(product, length, inverse):
    whole = jnp.round(product * inverse)
    return (product - whole * length) * inverse


def remote(source, target, send, receive, device):
    return pltpu.make_async_remote_copy(
        src_ref=source, dst_ref=target, send_sem=send, recv_sem=receive,
        device_id=device, device_id_type=MESH,
    )


def order_of(map_ref, wave, slot):
    return map_ref[wave * 2 + slot] * DEGREES // SLOTS


def whole_kernel(
    map_ref, len_ref, weight_ref, order_ref, leg_ref, spec_ref, spread_ref, gather_ref, natural_ref,
    grid_ref, out_ref,
    panel_ref, lhs, part, got, four, waves_ref, turned_ref, plain_ref, cross_ref, sum_ref,
    cos_ref, sin_ref, inner_ref, ret_ref, here, fields, piece, final,
    local_sem, chip_send, chip_recv, core_send, core_recv, coef_send, coef_recv, part_send, part_recv,
    wave_send, wave_recv, turn_send, turn_recv, line_send, line_recv, piece_send, piece_recv,
):
    wave = lax.axis_index("wave")
    lev = lax.axis_index("lev")
    line = lax.div(lev, LEAF)
    leaf = lax.rem(lev, LEAF)
    core = lax.rem(leaf, 2)
    chip = lax.div(leaf, 2)
    sibling = {"lev": lev + 1 - 2 * core}
    chips = [{"lev": line * LEAF + lax.rem(chip + d, 4) * 2 + core} for d in range(1, 4)]
    lines = [{"lev": lax.rem(line + d, LINES) * LEAF + leaf} for d in range(1, LINES)]
    waves = [{"wave": lax.rem(wave + d, WAVES)} for d in range(1, WAVES)]
    peers = waves + lines + chips + [sibling]
    barrier = pltpu.get_barrier_semaphore()
    for device in peers:
        pl.semaphore_signal(barrier, inc=1, device_id=device, device_id_type=MESH)

    first_lat = wave * OWN
    order_lane = order_ref[0:1, :]
    order_lane = order_lane + pltpu.roll(order_lane, 32, 1)
    order_lane = order_lane + pltpu.roll(order_lane, 64, 1)
    lane = lax.broadcasted_iota(jnp.int32, (1, LANES), 1)
    double = jnp.where(lane % SLOT_PAD < SLOTS, jnp.where(order_lane == 0.0, 1.0, 2.0), 0.0)
    order_sub = jnp.broadcast_to(order_lane, (LANES, LANES)).T[:SLOT_PAD]
    lane_f = lax.broadcasted_iota(jnp.int32, (ROWS_PAD, LANES), 1)
    row_f = lax.broadcasted_iota(jnp.int32, (ROWS_PAD, LANES), 0)
    block_start = (row_f // 2) * LANES
    position = block_start + lane_f
    block_start = block_start.astype(jnp.float32)
    second_lane = lane // SLOT_PAD % 2 == 1
    sign = jnp.where(lane < 64, 1.0, -1.0)
    inner_lane = lax.broadcasted_iota(jnp.int32, (SLOT_PAD, LANES), 1).astype(jnp.float32)
    inner_product = order_sub * inner_lane
    north = row_f % 2 == 0
    zero_block = jnp.zeros((SLOT_PAD, LANES), jnp.bfloat16)

    def tables(row):
        first_f = len_ref[first_lat + 2 * row].astype(jnp.float32)
        second_f = len_ref[first_lat + 2 * row + 1].astype(jnp.float32)
        length_lane = jnp.where(second_lane, second_f, first_f)
        start_lane = jnp.where(second_lane, first_f, 0.0)
        inverse_lane = 1.0 / length_lane
        inv_first = inverse_lane[:, 0:1]
        inv_second = inverse_lane[:, SLOT_PAD : SLOT_PAD + 1]
        outer = order_lane * (block_start - start_lane)
        outer_cos, outer_sin = cos_sin_turns(turns_of(outer, length_lane, inverse_lane))
        cos_ref[row] = outer_cos
        sin_ref[row] = outer_sin
        cos_a, sin_a = cos_sin_turns(turns_of(inner_product, first_f, inv_first))
        cos_b, sin_b = cos_sin_turns(turns_of(inner_product, second_f, inv_second))
        inner_ref[row] = jnp.concatenate(
            [
                jnp.concatenate([cos_a.astype(jnp.bfloat16), zero_block], 1),
                jnp.concatenate([zero_block, cos_b.astype(jnp.bfloat16)], 1),
                jnp.concatenate([(-sin_a).astype(jnp.bfloat16), zero_block], 1),
                jnp.concatenate([zero_block, (-sin_b).astype(jnp.bfloat16)], 1),
            ],
            0,
        )

    @pl.loop(0, EARLY_ROWS)
    def _(row):
        tables(row)

    pl.semaphore_wait(barrier, len(peers))

    copies = []

    def send(*details):
        copy = remote(*details)
        copy.start()
        copies.append(copy)

    for d in range(1, 4):
        send(leg_ref, panel_ref.at[leaf], chip_send.at[d - 1], chip_recv.at[d - 1], chips[d - 1])
    for d in range(1, LINES):
        send(spec_ref, lhs.at[line], coef_send.at[d - 1], coef_recv.at[d - 1], lines[d - 1])
    send(leg_ref, panel_ref.at[leaf], core_send.at[0], core_recv.at[0], sibling)
    own_panel = pltpu.make_async_copy(leg_ref, panel_ref.at[leaf], local_sem.at[0])
    own_panel.start()
    own_coef = pltpu.make_async_copy(spec_ref, lhs.at[line], local_sem.at[1])
    own_coef.start()

    @pl.loop(EARLY_ROWS, GRID_ROWS)
    def _(row):
        tables(row)

    width = panel_ref.shape[0] * panel_ref.shape[1]
    picked = lax.broadcasted_iota(jnp.int32, (DEGREES, width), 0) - line * SPAN
    widen = jnp.where(picked == lax.broadcasted_iota(jnp.int32, (DEGREES, width), 1) // 2, 1.0, 0.0)
    widen = widen.astype(jnp.bfloat16)
    four[...] = jnp.zeros_like(four)
    sum_ref[...] = jnp.zeros_like(sum_ref)
    for d in range(1, 4):
        block = panel_ref.at[lax.rem(chip + 4 - d, 4) * 2 + core]
        remote(block, block, chip_send.at[d - 1], chip_recv.at[d - 1], chips[d - 1]).wait_recv()
        send(block, block, core_send.at[d], core_recv.at[d], sibling)
    own_coef.wait()
    for d in range(1, LINES):
        block = lhs.at[lax.rem(line + LINES - d, LINES)]
        remote(block, block, coef_send.at[d - 1], coef_recv.at[d - 1], lines[d - 1]).wait_recv()
    coef = jnp.dot(lhs[...].reshape(LINES * 8, DEGREES), widen, preferred_element_type=jnp.float32)
    kind = lax.broadcasted_iota(jnp.int32, coef.shape, 0) % 8
    column = lax.broadcasted_iota(jnp.int32, coef.shape, 1)
    degree = column // 2 + line * SPAN
    order = jnp.where(kind >= 4, order_of(map_ref, wave, 1), order_of(map_ref, wave, 0))
    kept = (kind // 4 == column % 2) & (degree >= order)
    negated = (kind // 2 % 2 == 1) & ((degree + order) % 2 == 1)
    coef = jnp.where(kept, coef, 0.0)
    coef = jnp.where(negated, -coef, coef).astype(jnp.bfloat16)
    own_panel.wait()
    for d in range(4):
        block = panel_ref.at[lax.rem(chip + 4 - d, 4) * 2 + 1 - core]
        remote(block, block, core_send.at[d], core_recv.at[d], sibling).wait_recv()
    product = jnp.dot(coef, panel_ref[...].reshape(width, LATS), preferred_element_type=jnp.float32)
    part[...] = product.reshape(LINES, 8, LATS)
    for d in range(1, LINES):
        target = lax.rem(line + d, LINES)
        send(part.at[target], got.at[d - 1], part_send.at[d - 1], part_recv.at[d - 1], lines[d - 1])
    total = part[line]
    for d in range(1, LINES):
        block = got.at[d - 1]
        remote(block, block, part_send.at[d - 1], part_recv.at[d - 1], lines[d - 1]).wait_recv()
        total = total + got[d - 1]
    for w in range(WAVES):
        four[w, :, :OWN] = total[:, w * OWN : (w + 1) * OWN].astype(jnp.bfloat16)
    for d in range(1, WAVES):
        target = lax.rem(wave + d, WAVES)
        send(four.at[target], waves_ref.at[wave], wave_send.at[d - 1], wave_recv.at[d - 1], waves[d - 1])
    own_wave = pltpu.make_async_copy(four.at[wave], waves_ref.at[wave], local_sem.at[2])
    own_wave.start()
    own_wave.wait()
    for d in range(1, WAVES):
        block = waves_ref.at[lax.rem(wave + WAVES - d, WAVES)]
        remote(block, block, wave_send.at[d - 1], wave_recv.at[d - 1], waves[d - 1]).wait_recv()

    arrived = waves_ref[...].reshape(WAVES * 8, LANES)
    turned = lax.dot_general(
        arrived, spread_ref[...], (((0,), (0,)), ((), ())), preferred_element_type=jnp.float32
    )
    for h in range(2):
        turned_ref[...] = turned[:, h * LANES : (h + 1) * LANES]
        half = jnp.where(
            second_lane, turned_ref[pl.ds(1, CYCLE_PAD, 2), :], turned_ref[pl.ds(0, CYCLE_PAD, 2), :]
        )
        half = half * double
        plain_ref[h] = half
        cross_ref[h] = -sign * pltpu.roll(half, 64, 1)

    @pl.loop(0, GRID_ROWS)
    def _(row):
        first = len_ref[first_lat + 2 * row]
        second = len_ref[first_lat + 2 * row + 1]
        length_lane = jnp.where(second_lane, second.astype(jnp.float32), first.astype(jnp.float32))
        weight_lane = jnp.where(
            second_lane, weight_ref[first_lat + 2 * row + 1], weight_ref[first_lat + 2 * row]
        )
        resolved = 2.0 * order_lane < length_lane
        factor = jnp.where(resolved, weight_lane / length_lane, 0.0)
        inner = inner_ref[row]
        plain = jnp.where(north, plain_ref[0, pl.ds(row, 1), :], plain_ref[1, pl.ds(row, 1), :])
        crossed = jnp.where(north, cross_ref[0, pl.ds(row, 1), :], cross_ref[1, pl.ds(row, 1), :])
        spread = jnp.where(resolved, plain * cos_ref[row] + crossed * sin_ref[row], 0.0).astype(jnp.bfloat16)
        images = jnp.dot(spread, inner, preferred_element_type=jnp.float32)
        in_first = position < first
        occupied = position < first + second
        values = jnp.where(in_first, images[:, :LANES], jnp.where(occupied, images[:, LANES:], 0.0))
        values = values.astype(jnp.bfloat16)
        for block in range(BLOCKS):
            grid_ref[row, :, block * LANES : (block + 1) * LANES] = values[2 * block : 2 * block + 2]
        wide = values.astype(jnp.float32)
        squared = wide * wide
        by_cycle = jnp.concatenate(
            [
                jnp.where(in_first, squared, 0.0).astype(jnp.bfloat16),
                jnp.where(in_first, 0.0, squared).astype(jnp.bfloat16),
            ],
            1,
        )
        partial = lax.dot_general(by_cycle, inner, NT, preferred_element_type=jnp.float32)
        cos_sum = jnp.sum((partial * cos_ref[row]).reshape(ROWS_PAD // 8, 8, LANES), 0)
        sin_sum = jnp.sum((partial * sin_ref[row]).reshape(ROWS_PAD // 8, 8, LANES), 0)
        total = cos_sum + sign * pltpu.roll(sin_sum, 64, 1)
        total = total + pltpu.roll(total, 4, 0)
        total = total + pltpu.roll(total, 2, 0)
        sum_ref[0, pl.ds(row, 1), :] = total[0:1, :] * factor
        sum_ref[1, pl.ds(row, 1), :] = total[1:2, :] * factor

    sums = jnp.concatenate([sum_ref[0], sum_ref[1]], 1).astype(jnp.bfloat16)
    returned = jnp.concatenate(
        [
            lax.dot_general(gather_ref[cycle], sums, NT, preferred_element_type=jnp.float32)
            for cycle in range(2)
        ],
        1,
    )
    returned = jnp.dot(returned.astype(jnp.bfloat16), natural_ref[...], preferred_element_type=jnp.float32)
    ret_ref[...] = returned.astype(jnp.bfloat16).reshape(WAVES, 8, LANES)

    for d in range(1, WAVES):
        target = lax.rem(wave + d, WAVES)
        send(ret_ref.at[target], here.at[wave], turn_send.at[d - 1], turn_recv.at[d - 1], waves[d - 1])
    own_turn = pltpu.make_async_copy(ret_ref.at[wave], here.at[wave], local_sem.at[3])
    own_turn.start()
    own_turn.wait()
    for d in range(1, WAVES):
        block = here.at[lax.rem(wave + WAVES - d, WAVES)]
        remote(block, block, turn_send.at[d - 1], turn_recv.at[d - 1], waves[d - 1]).wait_recv()
    for d in range(1, LINES):
        send(here, fields.at[line], line_send.at[d - 1], line_recv.at[d - 1], lines[d - 1])
    own_line = pltpu.make_async_copy(here, fields.at[line], local_sem.at[4])
    own_line.start()
    own_line.wait()
    for d in range(1, LINES):
        block = fields.at[lax.rem(line + LINES - d, LINES)]
        remote(block, block, line_send.at[d - 1], line_recv.at[d - 1], lines[d - 1]).wait_recv()
    columns = jnp.concatenate(
        [fields[:, w].reshape(LINES * 8, LANES)[:, :OWN].astype(jnp.float32) for w in range(WAVES)], 1
    ).astype(jnp.bfloat16)
    product = lax.dot_general(
        columns, panel_ref[...].reshape(width, LATS), NT, preferred_element_type=jnp.float32
    )
    product = jnp.where(kept, product, 0.0)
    product = jnp.where(negated, -product, product)
    narrow = lax.broadcasted_iota(jnp.int32, (width, SPAN), 0) // 2 == lax.broadcasted_iota(jnp.int32, (width, SPAN), 1)
    product = jnp.dot(
        product, jnp.where(narrow, 1.0, 0.0), precision=lax.Precision.HIGHEST, preferred_element_type=jnp.float32
    )
    piece[...] = product.reshape(LINES, 8, SPAN)
    for d in range(1, LINES):
        target = lax.rem(line + d, LINES)
        send(piece.at[target], final.at[line], piece_send.at[d - 1], piece_recv.at[d - 1], lines[d - 1])
    own_piece = pltpu.make_async_copy(piece.at[line], final.at[line], local_sem.at[5])
    own_piece.start()
    own_piece.wait()
    for d in range(1, LINES):
        block = final.at[lax.rem(line + LINES - d, LINES)]
        remote(block, block, piece_send.at[d - 1], piece_recv.at[d - 1], lines[d - 1]).wait_recv()
    result = jnp.concatenate([final[y] for y in range(LINES)], 1)
    for s in range(2):
        out_ref[s] = result[4 * s : 4 * s + 2] + result[4 * s + 2 : 4 * s + 4]
    for copy in copies:
        copy.wait_send()


def per_device(spec, legendre, gauss_w, cycle_len, wave_map):
    slots_dev = spec.shape[0]
    depth = legendre.shape[1] * slots_dev
    panel = legendre.transpose(1, 0, 2).reshape(depth, LATS)
    doubled = jnp.broadcast_to(spec, (slots_dev, 2, 2, DEGREES)).reshape(8, DEGREES)
    orders = (wave_map * DEGREES // SLOTS).astype(jnp.float32)
    orders = jnp.broadcast_to(jnp.pad(orders, (0, LANES - SLOTS))[None, :], (8, LANES))

    line = np.arange(WAVES * 8)
    line_slot, line_half, line_part = line // 8 * 2 + line % 8 // 4, line // 2 % 2, line % 2
    both = np.arange(2 * LANES)
    both_half, both_part, both_cycle, both_slot = both // LANES, both // 64 % 2, both // 32 % 2, both % 32
    match = (
        (line_slot[:, None] == both_slot) & (line_half[:, None] == both_half) & (line_part[:, None] == both_part)
    )
    spread = jnp.asarray(match, jnp.bfloat16)
    packed = np.arange(LANES)
    natural = (packed % CYCLE_PAD < GRID_ROWS)[:, None] & (
        (packed % CYCLE_PAD * 2 + packed // CYCLE_PAD)[:, None] == packed[None, :]
    )
    natural = jnp.asarray(natural, jnp.bfloat16)
    gather = jnp.asarray(np.stack([match & (both_cycle == 0), match & (both_cycle == 1)]), jnp.bfloat16)

    vmem = pl.BlockSpec(memory_space=pltpu.VMEM)
    smem = pl.BlockSpec(memory_space=pltpu.SMEM)
    dma = pltpu.SemaphoreType.DMA
    bf16, f32 = jnp.bfloat16, jnp.float32
    grid, spec_out = pl.pallas_call(
        whole_kernel,
        out_shape=(
            jax.ShapeDtypeStruct((GRID_ROWS, 2, LPAD), bf16),
            jax.ShapeDtypeStruct((slots_dev, 2, DEGREES), f32),
        ),
        in_specs=[smem] * 3 + [vmem] * 6,
        out_specs=(vmem, vmem),
        scratch_shapes=[
            pltpu.VMEM((LEAF, depth, LATS), bf16),
            pltpu.VMEM((LINES, 8, DEGREES), bf16),
            pltpu.VMEM((LINES, 8, LATS), f32),
            pltpu.VMEM((LINES - 1, 8, LATS), f32),
            pltpu.VMEM((WAVES, 8, LANES), bf16),
            pltpu.VMEM((WAVES, 8, LANES), bf16),
            pltpu.VMEM((LANES, LANES), f32),
            pltpu.VMEM((2, CYCLE_PAD, LANES), f32),
            pltpu.VMEM((2, CYCLE_PAD, LANES), f32),
            pltpu.VMEM((2, CYCLE_PAD, LANES), f32),
            pltpu.VMEM((GRID_ROWS, ROWS_PAD, LANES), f32),
            pltpu.VMEM((GRID_ROWS, ROWS_PAD, LANES), f32),
            pltpu.VMEM((GRID_ROWS, LANES, 2 * LANES), bf16),
            pltpu.VMEM((WAVES, 8, LANES), bf16),
            pltpu.VMEM((WAVES, 8, LANES), bf16),
            pltpu.VMEM((LINES, WAVES, 8, LANES), bf16),
            pltpu.VMEM((LINES, 8, SPAN), f32),
            pltpu.VMEM((LINES, 8, SPAN), f32),
            dma((6,)), dma((3,)), dma((3,)), dma((4,)), dma((4,)),
            dma((LINES - 1,)), dma((LINES - 1,)), dma((LINES - 1,)), dma((LINES - 1,)),
            dma((WAVES - 1,)), dma((WAVES - 1,)), dma((WAVES - 1,)), dma((WAVES - 1,)),
            dma((LINES - 1,)), dma((LINES - 1,)), dma((LINES - 1,)), dma((LINES - 1,)),
        ],
        compiler_params=pltpu.CompilerParams(collective_id=0, has_side_effects=True),
        name="whole",
    )(wave_map, cycle_len, gauss_w, orders, panel, doubled, spread, gather, natural)
    grid = grid.transpose(1, 0, 2).reshape(2, GRID_ROWS, 1, LPAD)
    return (grid, spec_out.reshape(slots_dev, 1, 2, DEGREES))


def solution(mesh):
    placed = (P("wave", "lev", None, None), P("wave", "lev", None), P(), P(), P())
    return jax.shard_map(
        per_device,
        mesh=mesh,
        in_specs=placed,
        out_specs=(P(None, "wave", "lev", None), P("wave", "lev", None, None)),
        check_vma=False,
    )
```

time: 191 us -> 89.5 us (0.47)
  waiting for transfers between devices: 114 us -> 0 us
  Pallas kernels: 16.6 us -> 80.1 us
  between operations: 14.2 us -> 0.67 us
  starting transfers between devices: 13.4 us -> 0 us
  local copies, waits for them, and re-layouts: 19.1 us -> 6.26 us
  matrix products: 8.55 us -> 0 us
  other arithmetic: 3.76 us -> 0.67 us
    all_gather x1 -> x0, waiting for transfers between devices: 98.6 us -> none  [per_device(): panels = lax.all_gather(legendre, 'lev', axis=1, tiled=True)]
    pallas_call x1, Pallas kernels: 16.6 us -> 80.1 us  [per_device(): pl.pallas_call(whole_kernel, out_shape=(jax.ShapeDtypeStruct((GRID_ROWS,...]
    all_to_all x2 -> x0, waiting for transfers between devices: 14.9 us -> none  [the longest x1 9.03 us: per_device(): lax.all_to_all(fourier, 'wave', split_axis=4, concat_axis=0, tiled=True)]
    all_to_all x2 -> x0, starting transfers between devices: 13.3 us -> none  [the longest x1 9.9 us: per_device(): lax.all_to_all(fourier, 'wave', split_axis=4, concat_axis=0, tiled=True)]
    dot_general x2 -> x0, matrix products: 8.55 us -> none  [the longest x1 4.69 us: per_device(): jnp.einsum('shfcq,snq->shfcn', spectral, panels, preferred_element_type=j...]
    convert_element_type x5 -> x0, local copies, waits for them, and re-layouts: 4.49 us -> none  [the longest x1 2.61 us: per_device(): fourier = jnp.einsum('shfcn,snq->shfcq', stacked, panels, preferred_eleme...]
    reshape x6 -> x2, local copies, waits for them, and re-layouts: 5.11 us -> 2.22 us  [the longest x1 1.6 us: per_device(): panel = legendre.transpose(1, 0, 2).reshape(depth, LATS)]
    all_to_all x2 -> x0, local copies, waits for them, and re-layouts: 2.37 us -> none  [the longest x1 2.37 us: per_device(): lax.all_to_all(fourier, 'wave', split_axis=4, concat_axis=0, tiled=True)]
  transfers between devices with their start and end apart: 3 -> 0, of which waited for: 3 -> 0; matrix products, arithmetic and copies ran while one was open for 4% -> 0% of each run, Pallas kernels for 0% -> 0%
where the time goes in v4:
time: 89.5 us; the launch traced here: 87.7 us
  Pallas kernels  80.1 us (89%)
  local copies, waits for them, and re-layouts  6.26 us (7%)
    pallas_call x1, Pallas kernels, per_device(): pl.pallas_call(whole_kernel, out_shape=(jax.ShapeDtypeStruct((GRID_ROWS,...  80.1 us
    unnamed x6, local copies, waits for them, and re-layouts  3.43 us

profile of v4, /device:TPU:1, one launch (start us, length us, event | category | flops | bytes accessed | tf_op | source)
XLA Modules:
  0.0 87.7 jit_solution(522438711984530561)
XLA Ops:
  0.6 0.0 copy-start.1
  0.6 0.7 fusion
  1.3 0.6 broadcast_in_dim.6.order_ref
  1.9 0.0 copy-done.1
  1.9 0.6 reshape.18.spec_ref
  2.6 1.6 %reshape.17.leg_ref = bf16[40,1200]{1,0:T(8,128)(2,1)} reshape(bf16[20,2,1200]{2,1,0:T(2,128)(2,1)} %bitcast.11) | data formatting | bytes 192000 | tf_op jit(solution)/shard_map/reshape | solution.py:321
  4.2 80.1 %whole.1 = (bf16[50,2,4864]{2,1,0:T(2,128)(2,1)}, f32[2,2,1280]{2,1,0:T(2,128)}) custom-call(s32[24]{0:T(128)} %map_ref.1, s32[1200]{0:T(1024)} %len_ref.1, f32[1200]{0:T(1024)} %weight_ref.1, f32[8,128]{1,0:T(8,128)} %broadcast_in_dim.6.order_ref, bf16[40,1200]{1,0:T(8,128)(2,1)} %reshape.17.leg_ref, bf16[8,1280]{1,0:T(8,128)(2,1)} %reshape.18.spec_ref, ...), custom_call_target="tpu_custom_call" | custom-call | tf_op jit(solution)/shard_map/whole/pallas_call | solution.py:345
  84.3 0.0 copy-start
  84.3 2.8 %copy.14 = bf16[2,50,1,4864]{3,0,2,1:T(2,128)(2,1)} copy(bf16[2,50,1,4864]{3,0,2,1:T(2,128)(2,1)} %bitcast.10) | data formatting | bytes 1945600
  87.1 0.0 copy-done
  87.1 0.6 copy.15
  (2 shorter events, 0.0 us)
Async XLA Ops:
  0.6 1.3 %copy-start.1 = (bf16[2,1,2,1280]{3,2,1,0:T(2,128)(2,1)S(1)}, bf16[2,1,2,1280]{3,2,1,0:T(2,128)(2,1)}, u32[]{:S(2)}) copy-start(bf16[2,1,2,1280]{3,2,1,0:T(2,128)(2,1)} %param.8) | copy-start | bytes 30724
  84.3 2.8 %copy-start = (f32[2,2,1280]{2,1,0:T(2,128)S(1)}, f32[2,2,1280]{2,1,0:T(2,128)}, u32[]{:S(2)}) copy-start(f32[2,2,1280]{2,1,0:T(2,128)} %get-tuple-element.5) | copy-start | bytes 61444

commit v5 on v4

--- a/solution.py
+++ b/solution.py
@@ -21,9 +21,12 @@
 OWN = LATS // WAVES
 GRID_ROWS = OWN // 2
 DEGREES = 1280
-SPAN = DEGREES // LINES
+SPAN = DEGREES // LEAF
+RUN = SPAN // LINES
 SLOTS = 24
 EARLY_ROWS = 20
+STEP_ROWS = 10
+CUTS = ((0, 24), (24, 16))
 MESH = pl.DeviceIdType.MESH
 NT = (((1,), (1,)), ((), ()))
 
@@ -69,20 +72,17 @@
     grid_ref, out_ref,
     panel_ref, lhs, part, got, four, waves_ref, turned_ref, plain_ref, cross_ref, sum_ref,
     cos_ref, sin_ref, inner_ref, ret_ref, here, fields, piece, final,
-    local_sem, chip_send, chip_recv, core_send, core_recv, coef_send, coef_recv, part_send, part_recv,
+    local_sem, ring_send, ring_recv, coef_send, coef_recv, part_send, part_recv,
     wave_send, wave_recv, turn_send, turn_recv, line_send, line_recv, piece_send, piece_recv,
 ):
     wave = lax.axis_index("wave")
     lev = lax.axis_index("lev")
     line = lax.div(lev, LEAF)
     leaf = lax.rem(lev, LEAF)
-    core = lax.rem(leaf, 2)
-    chip = lax.div(leaf, 2)
-    sibling = {"lev": lev + 1 - 2 * core}
-    chips = [{"lev": line * LEAF + lax.rem(chip + d, 4) * 2 + core} for d in range(1, 4)]
-    lines = [{"lev": lax.rem(line + d, LINES) * LEAF + leaf} for d in range(1, LINES)]
+    ring = [{"lev": lax.rem(line + d, LINES) * LEAF + leaf} for d in (1, LINES - 1)]
+    leaves = [{"lev": line * LEAF + lax.rem(leaf + d, LEAF)} for d in range(1, LEAF)]
     waves = [{"wave": lax.rem(wave + d, WAVES)} for d in range(1, WAVES)]
-    peers = waves + lines + chips + [sibling]
+    peers = waves + leaves + ring
     barrier = pltpu.get_barrier_semaphore()
     for device in peers:
         pl.semaphore_signal(barrier, inc=1, device_id=device, device_id_type=MESH)
@@ -143,56 +143,71 @@
         copy.start()
         copies.append(copy)
 
-    for d in range(1, 4):
-        send(leg_ref, panel_ref.at[leaf], chip_send.at[d - 1], chip_recv.at[d - 1], chips[d - 1])
-    for d in range(1, LINES):
-        send(spec_ref, lhs.at[line], coef_send.at[d - 1], coef_recv.at[d - 1], lines[d - 1])
-    send(leg_ref, panel_ref.at[leaf], core_send.at[0], core_recv.at[0], sibling)
-    own_panel = pltpu.make_async_copy(leg_ref, panel_ref.at[leaf], local_sem.at[0])
+    def ring_copy(source, block, way, hop, cut):
+        start, size = CUTS[cut]
+        target = panel_ref.at[block, pl.ds(start, size), :]
+        return (
+            target if source is None else source.at[pl.ds(start, size), :],
+            target,
+            ring_send.at[way, hop - 1, cut],
+            ring_recv.at[way, hop - 1, cut],
+            ring[way],
+        )
+
+    for cut in range(2):
+        for way in range(2):
+            send(*ring_copy(leg_ref, line, way, 1, cut))
+    own_panel = pltpu.make_async_copy(leg_ref, panel_ref.at[line], local_sem.at[0])
     own_panel.start()
-    own_coef = pltpu.make_async_copy(spec_ref, lhs.at[line], local_sem.at[1])
+    for d in range(1, LEAF):
+        send(spec_ref, lhs.at[leaf], coef_send.at[d - 1], coef_recv.at[d - 1], leaves[d - 1])
+    own_coef = pltpu.make_async_copy(spec_ref, lhs.at[leaf], local_sem.at[1])
     own_coef.start()
 
-    @pl.loop(EARLY_ROWS, GRID_ROWS)
-    def _(row):
-        tables(row)
+    for hop in range(1, 4):
+
+        @pl.loop(EARLY_ROWS + (hop - 1) * STEP_ROWS, EARLY_ROWS + hop * STEP_ROWS)
+        def _(row):
+            tables(row)
+
+        for cut in range(2):
+            for way in range(2):
+                origin = lax.rem(line + (LINES - hop if way == 0 else hop), LINES)
+                remote(*ring_copy(None, origin, way, hop, cut)).wait_recv()
+                if hop < 3 or cut == way:
+                    send(*ring_copy(None, origin, way, hop + 1, cut))
 
     width = panel_ref.shape[0] * panel_ref.shape[1]
-    picked = lax.broadcasted_iota(jnp.int32, (DEGREES, width), 0) - line * SPAN
-    widen = jnp.where(picked == lax.broadcasted_iota(jnp.int32, (DEGREES, width), 1) // 2, 1.0, 0.0)
+    column = lax.broadcasted_iota(jnp.int32, (1, width), 1)
+    degree = column // (2 * RUN) * SPAN + leaf * RUN + column % (2 * RUN) // 2
+    widen = jnp.where(lax.broadcasted_iota(jnp.int32, (DEGREES, width), 0) == degree, 1.0, 0.0)
     widen = widen.astype(jnp.bfloat16)
     four[...] = jnp.zeros_like(four)
     sum_ref[...] = jnp.zeros_like(sum_ref)
-    for d in range(1, 4):
-        block = panel_ref.at[lax.rem(chip + 4 - d, 4) * 2 + core]
-        remote(block, block, chip_send.at[d - 1], chip_recv.at[d - 1], chips[d - 1]).wait_recv()
-        send(block, block, core_send.at[d], core_recv.at[d], sibling)
     own_coef.wait()
-    for d in range(1, LINES):
-        block = lhs.at[lax.rem(line + LINES - d, LINES)]
-        remote(block, block, coef_send.at[d - 1], coef_recv.at[d - 1], lines[d - 1]).wait_recv()
-    coef = jnp.dot(lhs[...].reshape(LINES * 8, DEGREES), widen, preferred_element_type=jnp.float32)
+    for d in range(1, LEAF):
+        block = lhs.at[lax.rem(leaf + LEAF - d, LEAF)]
+        remote(block, block, coef_send.at[d - 1], coef_recv.at[d - 1], leaves[d - 1]).wait_recv()
+    coef = jnp.dot(lhs[...].reshape(LEAF * 8, DEGREES), widen, preferred_element_type=jnp.float32)
     kind = lax.broadcasted_iota(jnp.int32, coef.shape, 0) % 8
-    column = lax.broadcasted_iota(jnp.int32, coef.shape, 1)
-    degree = column // 2 + line * SPAN
     order = jnp.where(kind >= 4, order_of(map_ref, wave, 1), order_of(map_ref, wave, 0))
     kept = (kind // 4 == column % 2) & (degree >= order)
     negated = (kind // 2 % 2 == 1) & ((degree + order) % 2 == 1)
     coef = jnp.where(kept, coef, 0.0)
     coef = jnp.where(negated, -coef, coef).astype(jnp.bfloat16)
     own_panel.wait()
-    for d in range(4):
-        block = panel_ref.at[lax.rem(chip + 4 - d, 4) * 2 + 1 - core]
-        remote(block, block, core_send.at[d], core_recv.at[d], sibling).wait_recv()
+    far = lax.rem(line + LINES // 2, LINES)
+    for cut in range(2):
+        remote(*ring_copy(None, far, cut, 4, cut)).wait_recv()
     product = jnp.dot(coef, panel_ref[...].reshape(width, LATS), preferred_element_type=jnp.float32)
-    part[...] = product.reshape(LINES, 8, LATS)
-    for d in range(1, LINES):
-        target = lax.rem(line + d, LINES)
-        send(part.at[target], got.at[d - 1], part_send.at[d - 1], part_recv.at[d - 1], lines[d - 1])
-    total = part[line]
-    for d in range(1, LINES):
+    part[...] = product.reshape(LEAF, 8, LATS)
+    for d in range(1, LEAF):
+        target = lax.rem(leaf + d, LEAF)
+        send(part.at[target], got.at[d - 1], part_send.at[d - 1], part_recv.at[d - 1], leaves[d - 1])
+    total = part[leaf]
+    for d in range(1, LEAF):
         block = got.at[d - 1]
-        remote(block, block, part_send.at[d - 1], part_recv.at[d - 1], lines[d - 1]).wait_recv()
+        remote(block, block, part_send.at[d - 1], part_recv.at[d - 1], leaves[d - 1]).wait_recv()
         total = total + got[d - 1]
     for w in range(WAVES):
         four[w, :, :OWN] = total[:, w * OWN : (w + 1) * OWN].astype(jnp.bfloat16)
@@ -278,16 +293,16 @@
     for d in range(1, WAVES):
         block = here.at[lax.rem(wave + WAVES - d, WAVES)]
         remote(block, block, turn_send.at[d - 1], turn_recv.at[d - 1], waves[d - 1]).wait_recv()
-    for d in range(1, LINES):
-        send(here, fields.at[line], line_send.at[d - 1], line_recv.at[d - 1], lines[d - 1])
-    own_line = pltpu.make_async_copy(here, fields.at[line], local_sem.at[4])
+    for d in range(1, LEAF):
+        send(here, fields.at[leaf], line_send.at[d - 1], line_recv.at[d - 1], leaves[d - 1])
+    own_line = pltpu.make_async_copy(here, fields.at[leaf], local_sem.at[4])
     own_line.start()
     own_line.wait()
-    for d in range(1, LINES):
-        block = fields.at[lax.rem(line + LINES - d, LINES)]
-        remote(block, block, line_send.at[d - 1], line_recv.at[d - 1], lines[d - 1]).wait_recv()
+    for d in range(1, LEAF):
+        block = fields.at[lax.rem(leaf + LEAF - d, LEAF)]
+        remote(block, block, line_send.at[d - 1], line_recv.at[d - 1], leaves[d - 1]).wait_recv()
     columns = jnp.concatenate(
-        [fields[:, w].reshape(LINES * 8, LANES)[:, :OWN].astype(jnp.float32) for w in range(WAVES)], 1
+        [fields[:, w].reshape(LEAF * 8, LANES)[:, :OWN].astype(jnp.float32) for w in range(WAVES)], 1
     ).astype(jnp.bfloat16)
     product = lax.dot_general(
         columns, panel_ref[...].reshape(width, LATS), NT, preferred_element_type=jnp.float32
@@ -298,17 +313,20 @@
     product = jnp.dot(
         product, jnp.where(narrow, 1.0, 0.0), precision=lax.Precision.HIGHEST, preferred_element_type=jnp.float32
     )
-    piece[...] = product.reshape(LINES, 8, SPAN)
-    for d in range(1, LINES):
-        target = lax.rem(line + d, LINES)
-        send(piece.at[target], final.at[line], piece_send.at[d - 1], piece_recv.at[d - 1], lines[d - 1])
-    own_piece = pltpu.make_async_copy(piece.at[line], final.at[line], local_sem.at[5])
+    piece[...] = product.reshape(LEAF, 8, SPAN)
+    for d in range(1, LEAF):
+        target = lax.rem(leaf + d, LEAF)
+        send(piece.at[target], final.at[leaf], piece_send.at[d - 1], piece_recv.at[d - 1], leaves[d - 1])
+    own_piece = pltpu.make_async_copy(piece.at[leaf], final.at[leaf], local_sem.at[5])
     own_piece.start()
     own_piece.wait()
-    for d in range(1, LINES):
-        block = final.at[lax.rem(line + LINES - d, LINES)]
-        remote(block, block, piece_send.at[d - 1], piece_recv.at[d - 1], lines[d - 1]).wait_recv()
-    result = jnp.concatenate([final[y] for y in range(LINES)], 1)
+    for d in range(1, LEAF):
+        block = final.at[lax.rem(leaf + LEAF - d, LEAF)]
+        remote(block, block, piece_send.at[d - 1], piece_recv.at[d - 1], leaves[d - 1]).wait_recv()
+    pieces = [final[k] for k in range(LEAF)]
+    result = jnp.concatenate(
+        [pieces[k][:, y * RUN : (y + 1) * RUN] for y in range(LINES) for k in range(LEAF)], 1
+    )
     for s in range(2):
         out_ref[s] = result[4 * s : 4 * s + 2] + result[4 * s + 2 : 4 * s + 4]
     for copy in copies:
@@ -351,10 +369,10 @@
         in_specs=[smem] * 3 + [vmem] * 6,
         out_specs=(vmem, vmem),
         scratch_shapes=[
-            pltpu.VMEM((LEAF, depth, LATS), bf16),
-            pltpu.VMEM((LINES, 8, DEGREES), bf16),
-            pltpu.VMEM((LINES, 8, LATS), f32),
-            pltpu.VMEM((LINES - 1, 8, LATS), f32),
+            pltpu.VMEM((LINES, depth, LATS), bf16),
+            pltpu.VMEM((LEAF, 8, DEGREES), bf16),
+            pltpu.VMEM((LEAF, 8, LATS), f32),
+            pltpu.VMEM((LEAF - 1, 8, LATS), f32),
             pltpu.VMEM((WAVES, 8, LANES), bf16),
             pltpu.VMEM((WAVES, 8, LANES), bf16),
             pltpu.VMEM((LANES, LANES), f32),
@@ -366,13 +384,13 @@
             pltpu.VMEM((GRID_ROWS, LANES, 2 * LANES), bf16),
             pltpu.VMEM((WAVES, 8, LANES), bf16),
             pltpu.VMEM((WAVES, 8, LANES), bf16),
-            pltpu.VMEM((LINES, WAVES, 8, LANES), bf16),
-            pltpu.VMEM((LINES, 8, SPAN), f32),
-            pltpu.VMEM((LINES, 8, SPAN), f32),
-            dma((6,)), dma((3,)), dma((3,)), dma((4,)), dma((4,)),
-            dma((LINES - 1,)), dma((LINES - 1,)), dma((LINES - 1,)), dma((LINES - 1,)),
+            pltpu.VMEM((LEAF, WAVES, 8, LANES), bf16),
+            pltpu.VMEM((LEAF, 8, SPAN), f32),
+            pltpu.VMEM((LEAF, 8, SPAN), f32),
+            dma((6,)), dma((2, 4, 2)), dma((2, 4, 2)),
+            dma((LEAF - 1,)), dma((LEAF - 1,)), dma((LEAF - 1,)), dma((LEAF - 1,)),
             dma((WAVES - 1,)), dma((WAVES - 1,)), dma((WAVES - 1,)), dma((WAVES - 1,)),
-            dma((LINES - 1,)), dma((LINES - 1,)), dma((LINES - 1,)), dma((LINES - 1,)),
+            dma((LEAF - 1,)), dma((LEAF - 1,)), dma((LEAF - 1,)), dma((LEAF - 1,)),
         ],
         compiler_params=pltpu.CompilerParams(collective_id=0, has_side_effects=True),
         name="whole",

time: 89.5 us -> 89 us (level); the launches traced: 87.7 us -> 88.8 us
  Pallas kernels: 80.1 us -> 81.2 us
    pallas_call x1, Pallas kernels: 80.1 us -> 81.2 us  [per_device(): pl.pallas_call(whole_kernel, out_shape=(jax.ShapeDtypeStruct((GRID_ROWS,...]
where the time goes in v5:
time: 89 us; the launch traced here: 88.8 us
  Pallas kernels  81.2 us (91%)
  local copies, waits for them, and re-layouts  6.26 us (7%)
    pallas_call x1, Pallas kernels, per_device(): pl.pallas_call(whole_kernel, out_shape=(jax.ShapeDtypeStruct((GRID_ROWS,...  81.2 us
    unnamed x6, local copies, waits for them, and re-layouts  3.43 us

profile of v5, /device:TPU:1, one launch (start us, length us, event | category | flops | bytes accessed | tf_op | source)
XLA Modules:
  0.0 88.8 jit_solution(11516381206873284496)
XLA Ops:
  0.6 0.0 copy-start.1
  0.6 0.7 fusion
  1.3 0.6 broadcast_in_dim.6.order_ref
  1.9 0.0 copy-done.1
  1.9 0.6 reshape.18.spec_ref
  2.6 1.6 %reshape.17.leg_ref = bf16[40,1200]{1,0:T(8,128)(2,1)} reshape(bf16[20,2,1200]{2,1,0:T(2,128)(2,1)} %bitcast.11) | data formatting | bytes 192000 | tf_op jit(solution)/shard_map/reshape | solution.py:339
  4.2 81.2 %whole.1 = (bf16[50,2,4864]{2,1,0:T(2,128)(2,1)}, f32[2,2,1280]{2,1,0:T(2,128)}) custom-call(s32[24]{0:T(128)} %map_ref.1, s32[1200]{0:T(1024)} %len_ref.1, f32[1200]{0:T(1024)} %weight_ref.1, f32[8,128]{1,0:T(8,128)} %broadcast_in_dim.6.order_ref, bf16[40,1200]{1,0:T(8,128)(2,1)} %reshape.17.leg_ref, bf16[8,1280]{1,0:T(8,128)(2,1)} %reshape.18.spec_ref, ...), custom_call_target="tpu_custom_call" | custom-call | tf_op jit(solution)/shard_map/whole/pallas_call | solution.py:363
  85.3 0.0 copy-start
  85.3 2.8 %copy.14 = bf16[2,50,1,4864]{3,0,2,1:T(2,128)(2,1)} copy(bf16[2,50,1,4864]{3,0,2,1:T(2,128)(2,1)} %bitcast.10) | data formatting | bytes 1945600
  88.2 0.0 copy-done
  88.2 0.6 copy.15
  (2 shorter events, 0.0 us)
Async XLA Ops:
  0.6 1.3 %copy-start.1 = (bf16[2,1,2,1280]{3,2,1,0:T(2,128)(2,1)S(1)}, bf16[2,1,2,1280]{3,2,1,0:T(2,128)(2,1)}, u32[]{:S(2)}) copy-start(bf16[2,1,2,1280]{3,2,1,0:T(2,128)(2,1)} %param.8) | copy-start | bytes 30724
  85.3 2.8 %copy-start = (f32[2,2,1280]{2,1,0:T(2,128)S(1)}, f32[2,2,1280]{2,1,0:T(2,128)}, u32[]{:S(2)}) copy-start(f32[2,2,1280]{2,1,0:T(2,128)} %get-tuple-element.5) | copy-start | bytes 61444

commit v6 on v5

--- a/solution.py
+++ b/solution.py
@@ -26,6 +26,7 @@
 SLOTS = 24
 EARLY_ROWS = 20
 STEP_ROWS = 10
+UNROLL = 5
 CUTS = ((0, 24), (24, 16))
 MESH = pl.DeviceIdType.MESH
 NT = (((1,), (1,)), ((), ()))
@@ -68,7 +69,7 @@
 
 
 def whole_kernel(
-    map_ref, len_ref, weight_ref, order_ref, leg_ref, spec_ref, spread_ref, gather_ref, natural_ref,
+    map_ref, len_ref, weight_ref, leg_ref, spec_ref, spread_ref, gather_ref, natural_ref,
     grid_ref, out_ref,
     panel_ref, lhs, part, got, four, waves_ref, turned_ref, plain_ref, cross_ref, sum_ref,
     cos_ref, sin_ref, inner_ref, ret_ref, here, fields, piece, final,
@@ -88,10 +89,11 @@
         pl.semaphore_signal(barrier, inc=1, device_id=device, device_id_type=MESH)
 
     first_lat = wave * OWN
-    order_lane = order_ref[0:1, :]
-    order_lane = order_lane + pltpu.roll(order_lane, 32, 1)
-    order_lane = order_lane + pltpu.roll(order_lane, 64, 1)
     lane = lax.broadcasted_iota(jnp.int32, (1, LANES), 1)
+    order_lane = jnp.zeros((1, LANES), jnp.int32)
+    for slot in range(SLOTS):
+        order_lane = jnp.where(lane % SLOT_PAD == slot, map_ref[slot] * DEGREES // SLOTS, order_lane)
+    order_lane = order_lane.astype(jnp.float32)
     double = jnp.where(lane % SLOT_PAD < SLOTS, jnp.where(order_lane == 0.0, 1.0, 2.0), 0.0)
     order_sub = jnp.broadcast_to(order_lane, (LANES, LANES)).T[:SLOT_PAD]
     lane_f = lax.broadcasted_iota(jnp.int32, (ROWS_PAD, LANES), 1)
@@ -234,8 +236,7 @@
         plain_ref[h] = half
         cross_ref[h] = -sign * pltpu.roll(half, 64, 1)
 
-    @pl.loop(0, GRID_ROWS)
-    def _(row):
+    def transform(row):
         first = len_ref[first_lat + 2 * row]
         second = len_ref[first_lat + 2 * row + 1]
         length_lane = jnp.where(second_lane, second.astype(jnp.float32), first.astype(jnp.float32))
@@ -273,6 +274,11 @@
         sum_ref[0, pl.ds(row, 1), :] = total[0:1, :] * factor
         sum_ref[1, pl.ds(row, 1), :] = total[1:2, :] * factor
 
+    @pl.loop(0, GRID_ROWS // UNROLL)
+    def _(step):
+        for near in range(UNROLL):
+            transform(step * UNROLL + near)
+
     sums = jnp.concatenate([sum_ref[0], sum_ref[1]], 1).astype(jnp.bfloat16)
     returned = jnp.concatenate(
         [
@@ -333,14 +339,25 @@
         copy.wait_send()
 
 
+def put_kernel(source, target, held, arrive, leave):
+    count, size = held.shape[0], held.shape[1]
+    spans = [pl.ds(part * size, size) for part in range(count)]
+    incoming = [pltpu.make_async_copy(source.at[spans[i]], held.at[i], arrive.at[i]) for i in range(count)]
+    outgoing = [pltpu.make_async_copy(held.at[i], target.at[spans[i]], leave.at[i]) for i in range(count)]
+    for copy in incoming:
+        copy.start()
+    for i in range(count):
+        incoming[i].wait()
+        outgoing[i].start()
+    for copy in outgoing:
+        copy.wait()
+
+
 def per_device(spec, legendre, gauss_w, cycle_len, wave_map):
     slots_dev = spec.shape[0]
     depth = legendre.shape[1] * slots_dev
     panel = legendre.transpose(1, 0, 2).reshape(depth, LATS)
     doubled = jnp.broadcast_to(spec, (slots_dev, 2, 2, DEGREES)).reshape(8, DEGREES)
-    orders = (wave_map * DEGREES // SLOTS).astype(jnp.float32)
-    orders = jnp.broadcast_to(jnp.pad(orders, (0, LANES - SLOTS))[None, :], (8, LANES))
-
     line = np.arange(WAVES * 8)
     line_slot, line_half, line_part = line // 8 * 2 + line % 8 // 4, line // 2 % 2, line % 2
     both = np.arange(2 * LANES)
@@ -366,7 +383,7 @@
             jax.ShapeDtypeStruct((GRID_ROWS, 2, LPAD), bf16),
             jax.ShapeDtypeStruct((slots_dev, 2, DEGREES), f32),
         ),
-        in_specs=[smem] * 3 + [vmem] * 6,
+        in_specs=[smem] * 3 + [vmem] * 5,
         out_specs=(vmem, vmem),
         scratch_shapes=[
             pltpu.VMEM((LINES, depth, LATS), bf16),
@@ -394,7 +411,16 @@
         ],
         compiler_params=pltpu.CompilerParams(collective_id=0, has_side_effects=True),
         name="whole",
-    )(wave_map, cycle_len, gauss_w, orders, panel, doubled, spread, gather, natural)
+    )(wave_map, cycle_len, gauss_w, panel, doubled, spread, gather, natural)
+    anywhere = pl.BlockSpec(memory_space=pl.ANY)
+    grid = pl.pallas_call(
+        put_kernel,
+        out_shape=jax.ShapeDtypeStruct(grid.shape, bf16),
+        in_specs=[anywhere],
+        out_specs=anywhere,
+        scratch_shapes=[pltpu.VMEM((5, GRID_ROWS // 5, 2, LPAD), bf16), dma((5,)), dma((5,))],
+        name="put",
+    )(grid)
     grid = grid.transpose(1, 0, 2).reshape(2, GRID_ROWS, 1, LPAD)
     return (grid, spec_out.reshape(slots_dev, 1, 2, DEGREES))
 

time: 89 us -> 75.9 us (0.85)
  Pallas kernels: 81.2 us -> 71.5 us
  local copies, waits for them, and re-layouts: 6.26 us -> 3.55 us
    pallas_call x1, Pallas kernels: 81.2 us -> 69.4 us  [per_device(): pl.pallas_call(whole_kernel, out_shape=(jax.ShapeDtypeStruct((GRID_ROWS,...]
    unnamed x6 -> x3, local copies, waits for them, and re-layouts: 3.43 us -> 0.61 us
    pallas_call x0 -> x1, Pallas kernels: none -> 2.05 us  [per_device(): pl.pallas_call(put_kernel, out_shape=jax.ShapeDtypeStruct(grid.shape, bf1...]
where the time goes in v6:
time: 75.9 us; the launch traced here: 75.7 us
  Pallas kernels  71.5 us (94%)
  local copies, waits for them, and re-layouts  3.55 us (5%)
    pallas_call x1, Pallas kernels, per_device(): pl.pallas_call(whole_kernel, out_shape=(jax.ShapeDtypeStruct((GRID_ROWS,...  69.4 us
    pallas_call x1, Pallas kernels, per_device(): pl.pallas_call(put_kernel, out_shape=jax.ShapeDtypeStruct(grid.shape, bf1...  2.05 us
    reshape x1, local copies, waits for them, and re-layouts, per_device(): panel = legendre.transpose(1, 0, 2).reshape(depth, LATS)  1.6 us

profile of v6, /device:TPU:1, one launch (start us, length us, event | category | flops | bytes accessed | tf_op | source)
XLA Modules:
  0.0 75.7 jit_solution(12449877680685072563)
XLA Ops:
  0.6 0.7 broadcast_in_dim.8
  1.3 0.6 reshape.17.spec_ref
  2.0 1.6 %reshape.16.leg_ref = bf16[40,1200]{1,0:T(8,128)(2,1)} reshape(bf16[20,2,1200]{2,1,0:T(2,128)(2,1)} %bitcast.11) | data formatting | bytes 192000 | tf_op jit(solution)/shard_map/reshape | solution.py:359
  3.6 69.4 %whole.1 = (bf16[50,2,4864]{2,1,0:T(2,128)(2,1)}, f32[2,2,1280]{2,1,0:T(2,128)}) custom-call(s32[24]{0:T(128)} %map_ref.1, s32[1200]{0:T(1024)} %len_ref.1, f32[1200]{0:T(1024)} %weight_ref.1, bf16[40,1200]{1,0:T(8,128)(2,1)} %reshape.16.leg_ref, bf16[8,1280]{1,0:T(8,128)(2,1)} %reshape.17.spec_ref, bf16[96,256]{1,0:T(8,128)(2,1)} %constant.6.clone.spread_ref, ...), custom_call_target="tpu_custom_call" | custom-call | tf_op jit(solution)/shard_map/whole/pallas_call | solution.py:380
  73.0 0.0 copy-start
  73.0 2.0 %put.1 = bf16[50,2,4864]{2,1,0:T(2,128)(2,1)} custom-call(bf16[50,2,4864]{2,1,0:T(2,128)(2,1)} %get-tuple-element.4.source), custom_call_target="tpu_custom_call" | custom-call | tf_op jit(solution)/shard_map/put/pallas_call | solution.py:416
  75.1 0.0 copy-done
  75.1 0.6 copy.13
Async XLA Ops:
  73.0 2.1 %copy-start = (f32[2,2,1280]{2,1,0:T(2,128)S(1)}, f32[2,2,1280]{2,1,0:T(2,128)}, u32[]{:S(2)}) copy-start(f32[2,2,1280]{2,1,0:T(2,128)} %get-tuple-element.5) | copy-start | bytes 61444

commit v7 on v6

--- a/solution.py
+++ b/solution.py
@@ -26,8 +26,9 @@
 SLOTS = 24
 EARLY_ROWS = 20
 STEP_ROWS = 10
-UNROLL = 5
-CUTS = ((0, 24), (24, 16))
+UNROLL = 10
+TABLE_UNROLL = 1
+CUTS = tuple((start, 8) for start in range(0, 40, 8))
 MESH = pl.DeviceIdType.MESH
 NT = (((1,), (1,)), ((), ()))
 
@@ -69,9 +70,9 @@
 
 
 def whole_kernel(
-    map_ref, len_ref, weight_ref, leg_ref, spec_ref, spread_ref, gather_ref, natural_ref,
+    map_ref, len_ref, weight_ref, stored_leg_ref, stored_spec_ref, spread_ref, gather_ref, natural_ref,
     grid_ref, out_ref,
-    panel_ref, lhs, part, got, four, waves_ref, turned_ref, plain_ref, cross_ref, sum_ref,
+    leg_ref, spec_ref, panel_ref, lhs, part, got, four, waves_ref, turned_ref, plain_ref, cross_ref, sum_ref,
     cos_ref, sin_ref, inner_ref, ret_ref, here, fields, piece, final,
     local_sem, ring_send, ring_recv, coef_send, coef_recv, part_send, part_recv,
     wave_send, wave_recv, turn_send, turn_recv, line_send, line_recv, piece_send, piece_recv,
@@ -87,6 +88,12 @@
     barrier = pltpu.get_barrier_semaphore()
     for device in peers:
         pl.semaphore_signal(barrier, inc=1, device_id=device, device_id_type=MESH)
+
+    for n in range(RUN):
+        leg_ref[2 * n : 2 * n + 2, :] = stored_leg_ref[n]
+    for s in range(2):
+        for h in range(2):
+            spec_ref[4 * s + 2 * h : 4 * s + 2 * h + 2, :] = stored_spec_ref[s]
 
     first_lat = wave * OWN
     lane = lax.broadcasted_iota(jnp.int32, (1, LANES), 1)
@@ -132,9 +139,13 @@
             0,
         )
 
-    @pl.loop(0, EARLY_ROWS)
-    def _(row):
-        tables(row)
+    def table_rows(start, count):
+        @pl.loop(0, count // TABLE_UNROLL)
+        def _(step):
+            for near in range(TABLE_UNROLL):
+                tables(start + step * TABLE_UNROLL + near)
+
+    table_rows(0, EARLY_ROWS)
 
     pl.semaphore_wait(barrier, len(peers))
 
@@ -156,7 +167,7 @@
             ring[way],
         )
 
-    for cut in range(2):
+    for cut in range(len(CUTS)):
         for way in range(2):
             send(*ring_copy(leg_ref, line, way, 1, cut))
     own_panel = pltpu.make_async_copy(leg_ref, panel_ref.at[line], local_sem.at[0])
@@ -167,16 +178,13 @@
     own_coef.start()
 
     for hop in range(1, 4):
-
-        @pl.loop(EARLY_ROWS + (hop - 1) * STEP_ROWS, EARLY_ROWS + hop * STEP_ROWS)
-        def _(row):
-            tables(row)
-
-        for cut in range(2):
+        if hop == 1:
+            table_rows(EARLY_ROWS, STEP_ROWS)
+        for cut in range(len(CUTS)):
             for way in range(2):
                 origin = lax.rem(line + (LINES - hop if way == 0 else hop), LINES)
                 remote(*ring_copy(None, origin, way, hop, cut)).wait_recv()
-                if hop < 3 or cut == way:
+                if hop < 3 or cut % 2 == way:
                     send(*ring_copy(None, origin, way, hop + 1, cut))
 
     width = panel_ref.shape[0] * panel_ref.shape[1]
@@ -199,13 +207,14 @@
     coef = jnp.where(negated, -coef, coef).astype(jnp.bfloat16)
     own_panel.wait()
     far = lax.rem(line + LINES // 2, LINES)
-    for cut in range(2):
-        remote(*ring_copy(None, far, cut, 4, cut)).wait_recv()
+    for cut in range(len(CUTS)):
+        remote(*ring_copy(None, far, cut % 2, 4, cut)).wait_recv()
     product = jnp.dot(coef, panel_ref[...].reshape(width, LATS), preferred_element_type=jnp.float32)
     part[...] = product.reshape(LEAF, 8, LATS)
     for d in range(1, LEAF):
         target = lax.rem(leaf + d, LEAF)
         send(part.at[target], got.at[d - 1], part_send.at[d - 1], part_recv.at[d - 1], leaves[d - 1])
+    table_rows(EARLY_ROWS + STEP_ROWS, STEP_ROWS)
     total = part[leaf]
     for d in range(1, LEAF):
         block = got.at[d - 1]
@@ -218,6 +227,7 @@
         send(four.at[target], waves_ref.at[wave], wave_send.at[d - 1], wave_recv.at[d - 1], waves[d - 1])
     own_wave = pltpu.make_async_copy(four.at[wave], waves_ref.at[wave], local_sem.at[2])
     own_wave.start()
+    table_rows(EARLY_ROWS + 2 * STEP_ROWS, STEP_ROWS)
     own_wave.wait()
     for d in range(1, WAVES):
         block = waves_ref.at[lax.rem(wave + WAVES - d, WAVES)]
@@ -356,8 +366,8 @@
 def per_device(spec, legendre, gauss_w, cycle_len, wave_map):
     slots_dev = spec.shape[0]
     depth = legendre.shape[1] * slots_dev
-    panel = legendre.transpose(1, 0, 2).reshape(depth, LATS)
-    doubled = jnp.broadcast_to(spec, (slots_dev, 2, 2, DEGREES)).reshape(8, DEGREES)
+    panel = legendre.transpose(1, 0, 2)
+    coefficients = spec.reshape(slots_dev, 2, DEGREES)
     line = np.arange(WAVES * 8)
     line_slot, line_half, line_part = line // 8 * 2 + line % 8 // 4, line // 2 % 2, line % 2
     both = np.arange(2 * LANES)
@@ -386,6 +396,8 @@
         in_specs=[smem] * 3 + [vmem] * 5,
         out_specs=(vmem, vmem),
         scratch_shapes=[
+            pltpu.VMEM((depth, LATS), bf16),
+            pltpu.VMEM((8, DEGREES), bf16),
             pltpu.VMEM((LINES, depth, LATS), bf16),
             pltpu.VMEM((LEAF, 8, DEGREES), bf16),
             pltpu.VMEM((LEAF, 8, LATS), f32),
@@ -404,14 +416,14 @@
             pltpu.VMEM((LEAF, WAVES, 8, LANES), bf16),
             pltpu.VMEM((LEAF, 8, SPAN), f32),
             pltpu.VMEM((LEAF, 8, SPAN), f32),
-            dma((6,)), dma((2, 4, 2)), dma((2, 4, 2)),
+            dma((6,)), dma((2, 4, len(CUTS))), dma((2, 4, len(CUTS))),
             dma((LEAF - 1,)), dma((LEAF - 1,)), dma((LEAF - 1,)), dma((LEAF - 1,)),
             dma((WAVES - 1,)), dma((WAVES - 1,)), dma((WAVES - 1,)), dma((WAVES - 1,)),
             dma((LEAF - 1,)), dma((LEAF - 1,)), dma((LEAF - 1,)), dma((LEAF - 1,)),
         ],
         compiler_params=pltpu.CompilerParams(collective_id=0, has_side_effects=True),
         name="whole",
-    )(wave_map, cycle_len, gauss_w, panel, doubled, spread, gather, natural)
+    )(wave_map, cycle_len, gauss_w, panel, coefficients, spread, gather, natural)
     anywhere = pl.BlockSpec(memory_space=pl.ANY)
     grid = pl.pallas_call(
         put_kernel,

time: 75.9 us -> 71.8 us (0.946)
  local copies, waits for them, and re-layouts: 3.55 us -> 0.61 us
  Pallas kernels: 71.5 us -> 70.3 us
    reshape x2 -> x0, local copies, waits for them, and re-layouts: 2.22 us -> none  [the longest x1 1.6 us: per_device(): panel = legendre.transpose(1, 0, 2).reshape(depth, LATS)]
    pallas_call x1, Pallas kernels: 69.4 us -> 68.3 us  [per_device(): pl.pallas_call(whole_kernel, out_shape=(jax.ShapeDtypeStruct((GRID_ROWS,...]
where the time goes in v7:
time: 71.8 us; the launch traced here: 71.6 us
  Pallas kernels  70.3 us (98%)
    pallas_call x1, Pallas kernels, per_device(): pl.pallas_call(whole_kernel, out_shape=(jax.ShapeDtypeStruct((GRID_ROWS,...  68.3 us
    pallas_call x1, Pallas kernels, per_device(): pl.pallas_call(put_kernel, out_shape=jax.ShapeDtypeStruct(grid.shape, bf1...  2.05 us

profile of v7, /device:TPU:1, one launch (start us, length us, event | category | flops | bytes accessed | tf_op | source)
XLA Modules:
  0.0 71.6 jit_solution(12227337075224056528)
XLA Ops:
  0.6 68.3 %whole.1 = (bf16[50,2,4864]{2,1,0:T(2,128)(2,1)}, f32[2,2,1280]{2,1,0:T(2,128)}) custom-call(s32[24]{0:T(128)} %map_ref.1, s32[1200]{0:T(1024)} %len_ref.1, f32[1200]{0:T(1024)} %weight_ref.1, bf16[20,2,1200]{2,1,0:T(2,128)(2,1)} %bitcast.11, bf16[2,2,1280]{2,1,0:T(2,128)(2,1)} %bitcast.13, bf16[96,256]{1,0:T(8,128)(2,1)} %constant.6.clone.spread_ref, ...), custom_call_target="tpu_custom_call" | custom-call | tf_op jit(solution)/shard_map/whole/pallas_call | solution.py:390
  68.9 0.0 copy-start
  68.9 2.0 %put.1 = bf16[50,2,4864]{2,1,0:T(2,128)(2,1)} custom-call(bf16[50,2,4864]{2,1,0:T(2,128)(2,1)} %get-tuple-element.4.source), custom_call_target="tpu_custom_call" | custom-call | tf_op jit(solution)/shard_map/put/pallas_call | solution.py:428
  71.0 0.0 copy-done
  71.0 0.6 copy.13
Async XLA Ops:
  68.9 2.1 %copy-start = (f32[2,2,1280]{2,1,0:T(2,128)S(1)}, f32[2,2,1280]{2,1,0:T(2,128)}, u32[]{:S(2)}) copy-start(f32[2,2,1280]{2,1,0:T(2,128)} %get-tuple-element.5) | copy-start | bytes 61444

commit v8 on v7

--- a/solution.py
+++ b/solution.py
@@ -29,6 +29,8 @@
 UNROLL = 10
 TABLE_UNROLL = 1
 CUTS = tuple((start, 8) for start in range(0, 40, 8))
+FAR_LEAVES = (4, 3, 5, 2, 6, 1, 7)
+FAR_WAVES = (6, 5, 7, 4, 8, 3, 9, 2, 10, 1, 11)
 MESH = pl.DeviceIdType.MESH
 NT = (((1,), (1,)), ((), ()))
 
@@ -71,8 +73,8 @@
 
 def whole_kernel(
     map_ref, len_ref, weight_ref, stored_leg_ref, stored_spec_ref, spread_ref, gather_ref, natural_ref,
-    grid_ref, out_ref,
-    leg_ref, spec_ref, panel_ref, lhs, part, got, four, waves_ref, turned_ref, plain_ref, cross_ref, sum_ref,
+    grid_out_ref, out_ref,
+    grid_ref, leg_ref, spec_ref, panel_ref, lhs, part, got, four, waves_ref, turned_ref, plain_ref, cross_ref, sum_ref,
     cos_ref, sin_ref, inner_ref, ret_ref, here, fields, piece, final,
     local_sem, ring_send, ring_recv, coef_send, coef_recv, part_send, part_recv,
     wave_send, wave_recv, turn_send, turn_recv, line_send, line_recv, piece_send, piece_recv,
@@ -211,7 +213,7 @@
         remote(*ring_copy(None, far, cut % 2, 4, cut)).wait_recv()
     product = jnp.dot(coef, panel_ref[...].reshape(width, LATS), preferred_element_type=jnp.float32)
     part[...] = product.reshape(LEAF, 8, LATS)
-    for d in range(1, LEAF):
+    for d in FAR_LEAVES:
         target = lax.rem(leaf + d, LEAF)
         send(part.at[target], got.at[d - 1], part_send.at[d - 1], part_recv.at[d - 1], leaves[d - 1])
     table_rows(EARLY_ROWS + STEP_ROWS, STEP_ROWS)
@@ -222,7 +224,7 @@
         total = total + got[d - 1]
     for w in range(WAVES):
         four[w, :, :OWN] = total[:, w * OWN : (w + 1) * OWN].astype(jnp.bfloat16)
-    for d in range(1, WAVES):
+    for d in FAR_WAVES:
         target = lax.rem(wave + d, WAVES)
         send(four.at[target], waves_ref.at[wave], wave_send.at[d - 1], wave_recv.at[d - 1], waves[d - 1])
     own_wave = pltpu.make_async_copy(four.at[wave], waves_ref.at[wave], local_sem.at[2])
@@ -289,6 +291,8 @@
         for near in range(UNROLL):
             transform(step * UNROLL + near)
 
+    own_grid = pltpu.make_async_copy(grid_ref, grid_out_ref, local_sem.at[6])
+    own_grid.start()
     sums = jnp.concatenate([sum_ref[0], sum_ref[1]], 1).astype(jnp.bfloat16)
     returned = jnp.concatenate(
         [
@@ -300,7 +304,7 @@
     returned = jnp.dot(returned.astype(jnp.bfloat16), natural_ref[...], preferred_element_type=jnp.float32)
     ret_ref[...] = returned.astype(jnp.bfloat16).reshape(WAVES, 8, LANES)
 
-    for d in range(1, WAVES):
+    for d in FAR_WAVES:
         target = lax.rem(wave + d, WAVES)
         send(ret_ref.at[target], here.at[wave], turn_send.at[d - 1], turn_recv.at[d - 1], waves[d - 1])
     own_turn = pltpu.make_async_copy(ret_ref.at[wave], here.at[wave], local_sem.at[3])
@@ -309,7 +313,7 @@
     for d in range(1, WAVES):
         block = here.at[lax.rem(wave + WAVES - d, WAVES)]
         remote(block, block, turn_send.at[d - 1], turn_recv.at[d - 1], waves[d - 1]).wait_recv()
-    for d in range(1, LEAF):
+    for d in FAR_LEAVES:
         send(here, fields.at[leaf], line_send.at[d - 1], line_recv.at[d - 1], leaves[d - 1])
     own_line = pltpu.make_async_copy(here, fields.at[leaf], local_sem.at[4])
     own_line.start()
@@ -330,7 +334,7 @@
         product, jnp.where(narrow, 1.0, 0.0), precision=lax.Precision.HIGHEST, preferred_element_type=jnp.float32
     )
     piece[...] = product.reshape(LEAF, 8, SPAN)
-    for d in range(1, LEAF):
+    for d in FAR_LEAVES:
         target = lax.rem(leaf + d, LEAF)
         send(piece.at[target], final.at[leaf], piece_send.at[d - 1], piece_recv.at[d - 1], leaves[d - 1])
     own_piece = pltpu.make_async_copy(piece.at[leaf], final.at[leaf], local_sem.at[5])
@@ -347,16 +351,19 @@
         out_ref[s] = result[4 * s : 4 * s + 2] + result[4 * s + 2 : 4 * s + 4]
     for copy in copies:
         copy.wait_send()
-
-
-def put_kernel(source, target, held, arrive, leave):
+    own_grid.wait()
+
+
+def put_kernel(source, small_source, target, small_target, held, small, arrive, leave):
     count, size = held.shape[0], held.shape[1]
     spans = [pl.ds(part * size, size) for part in range(count)]
     incoming = [pltpu.make_async_copy(source.at[spans[i]], held.at[i], arrive.at[i]) for i in range(count)]
     outgoing = [pltpu.make_async_copy(held.at[i], target.at[spans[i]], leave.at[i]) for i in range(count)]
+    incoming.append(pltpu.make_async_copy(small_source, small, arrive.at[count]))
+    outgoing.append(pltpu.make_async_copy(small, small_target, leave.at[count]))
     for copy in incoming:
         copy.start()
-    for i in range(count):
+    for i in range(count + 1):
         incoming[i].wait()
         outgoing[i].start()
     for copy in outgoing:
@@ -385,6 +392,7 @@
 
     vmem = pl.BlockSpec(memory_space=pltpu.VMEM)
     smem = pl.BlockSpec(memory_space=pltpu.SMEM)
+    anywhere = pl.BlockSpec(memory_space=pl.ANY)
     dma = pltpu.SemaphoreType.DMA
     bf16, f32 = jnp.bfloat16, jnp.float32
     grid, spec_out = pl.pallas_call(
@@ -394,8 +402,9 @@
             jax.ShapeDtypeStruct((slots_dev, 2, DEGREES), f32),
         ),
         in_specs=[smem] * 3 + [vmem] * 5,
-        out_specs=(vmem, vmem),
+        out_specs=(anywhere, vmem),
         scratch_shapes=[
+            pltpu.VMEM((GRID_ROWS, 2, LPAD), bf16),
             pltpu.VMEM((depth, LATS), bf16),
             pltpu.VMEM((8, DEGREES), bf16),
             pltpu.VMEM((LINES, depth, LATS), bf16),
@@ -416,7 +425,7 @@
             pltpu.VMEM((LEAF, WAVES, 8, LANES), bf16),
             pltpu.VMEM((LEAF, 8, SPAN), f32),
             pltpu.VMEM((LEAF, 8, SPAN), f32),
-            dma((6,)), dma((2, 4, len(CUTS))), dma((2, 4, len(CUTS))),
+            dma((7,)), dma((2, 4, len(CUTS))), dma((2, 4, len(CUTS))),
             dma((LEAF - 1,)), dma((LEAF - 1,)), dma((LEAF - 1,)), dma((LEAF - 1,)),
             dma((WAVES - 1,)), dma((WAVES - 1,)), dma((WAVES - 1,)), dma((WAVES - 1,)),
             dma((LEAF - 1,)), dma((LEAF - 1,)), dma((LEAF - 1,)), dma((LEAF - 1,)),
@@ -424,15 +433,21 @@
         compiler_params=pltpu.CompilerParams(collective_id=0, has_side_effects=True),
         name="whole",
     )(wave_map, cycle_len, gauss_w, panel, coefficients, spread, gather, natural)
-    anywhere = pl.BlockSpec(memory_space=pl.ANY)
-    grid = pl.pallas_call(
+    grid, spec_out = pl.pallas_call(
         put_kernel,
-        out_shape=jax.ShapeDtypeStruct(grid.shape, bf16),
-        in_specs=[anywhere],
-        out_specs=anywhere,
-        scratch_shapes=[pltpu.VMEM((5, GRID_ROWS // 5, 2, LPAD), bf16), dma((5,)), dma((5,))],
+        out_shape=(
+            jax.ShapeDtypeStruct(grid.shape, bf16),
+            jax.ShapeDtypeStruct(spec_out.shape, f32),
+        ),
+        in_specs=[anywhere] * 2,
+        out_specs=(anywhere,) * 2,
+        scratch_shapes=[
+            pltpu.VMEM((5, GRID_ROWS // 5, 2, LPAD), bf16),
+            pltpu.VMEM(spec_out.shape, f32),
+            dma((6,)), dma((6,)),
+        ],
         name="put",
-    )(grid)
+    )(grid, spec_out)
     grid = grid.transpose(1, 0, 2).reshape(2, GRID_ROWS, 1, LPAD)
     return (grid, spec_out.reshape(slots_dev, 1, 2, DEGREES))
 

time: 71.8 us -> 70.1 us (0.976)
  Pallas kernels: 70.3 us -> 69.2 us
    pallas_call x1, Pallas kernels: 68.3 us -> 67.2 us  [per_device(): pl.pallas_call(whole_kernel, out_shape=(jax.ShapeDtypeStruct((GRID_ROWS,...]
where the time goes in v8:
time: 70.1 us; the launch traced here: 69.9 us
  Pallas kernels  69.2 us (99%)
    pallas_call x1, Pallas kernels, per_device(): pl.pallas_call(whole_kernel, out_shape=(jax.ShapeDtypeStruct((GRID_ROWS,...  67.2 us
    pallas_call x1, Pallas kernels, per_device(): pl.pallas_call(put_kernel, out_shape=(jax.ShapeDtypeStruct(grid.shape, bf...  2.06 us

profile of v8, /device:TPU:1, one launch (start us, length us, event | category | flops | bytes accessed | tf_op | source)
XLA Modules:
  0.0 69.9 jit_solution(1667842442866701744)
XLA Ops:
  0.6 67.2 %whole.1 = (bf16[50,2,4864]{2,1,0:T(2,128)(2,1)}, f32[2,2,1280]{2,1,0:T(2,128)}) custom-call(s32[24]{0:T(128)} %map_ref.1, s32[1200]{0:T(1024)} %len_ref.1, f32[1200]{0:T(1024)} %weight_ref.1, bf16[20,2,1200]{2,1,0:T(2,128)(2,1)} %bitcast.10, bf16[2,2,1280]{2,1,0:T(2,128)(2,1)} %bitcast.11, bf16[96,256]{1,0:T(8,128)(2,1)} %constant.6.clone.spread_ref, ...), custom_call_target="tpu_custom_call" | custom-call | tf_op jit(solution)/shard_map/whole/pallas_call | solution.py:398
  67.8 2.1 %put.1 = (bf16[50,2,4864]{2,1,0:T(2,128)(2,1)}, f32[2,2,1280]{2,1,0:T(2,128)}) custom-call(bf16[50,2,4864]{2,1,0:T(2,128)(2,1)} %get-tuple-element.6.source, f32[2,2,1280]{2,1,0:T(2,128)} %get-tuple-element.7.small_source), custom_call_target="tpu_custom_call" | custom-call | tf_op jit(solution)/shard_map/put/pallas_call | solution.py:436

commit v9 on v8

--- a/solution.py
+++ b/solution.py
@@ -29,6 +29,7 @@
 UNROLL = 10
 TABLE_UNROLL = 1
 CUTS = tuple((start, 8) for start in range(0, 40, 8))
+SIDES = ((0, 640), (640, 560))
 FAR_LEAVES = (4, 3, 5, 2, 6, 1, 7)
 FAR_WAVES = (6, 5, 7, 4, 8, 3, 9, 2, 10, 1, 11)
 MESH = pl.DeviceIdType.MESH
@@ -211,17 +212,31 @@
     far = lax.rem(line + LINES // 2, LINES)
     for cut in range(len(CUTS)):
         remote(*ring_copy(None, far, cut % 2, 4, cut)).wait_recv()
-    product = jnp.dot(coef, panel_ref[...].reshape(width, LATS), preferred_element_type=jnp.float32)
-    part[...] = product.reshape(LEAF, 8, LATS)
-    for d in FAR_LEAVES:
-        target = lax.rem(leaf + d, LEAF)
-        send(part.at[target], got.at[d - 1], part_send.at[d - 1], part_recv.at[d - 1], leaves[d - 1])
+    for side, (low, size) in enumerate(SIDES):
+        span = pl.ds(low, size)
+        product = jnp.dot(
+            coef, panel_ref[:, :, low : low + size].reshape(width, size), preferred_element_type=jnp.float32
+        )
+        part[:, :, low : low + size] = product.reshape(LEAF, 8, size)
+        for d in FAR_LEAVES:
+            target = lax.rem(leaf + d, LEAF)
+            send(
+                part.at[target, :, span], got.at[d - 1, :, span],
+                part_send.at[side, d - 1], part_recv.at[side, d - 1], leaves[d - 1],
+            )
     table_rows(EARLY_ROWS + STEP_ROWS, STEP_ROWS)
-    total = part[leaf]
-    for d in range(1, LEAF):
-        block = got.at[d - 1]
-        remote(block, block, part_send.at[d - 1], part_recv.at[d - 1], leaves[d - 1]).wait_recv()
-        total = total + got[d - 1]
+    total = []
+    for side, (low, size) in enumerate(SIDES):
+        span = pl.ds(low, size)
+        piece_sum = part[leaf, :, low : low + size]
+        for d in range(1, LEAF):
+            block = got.at[d - 1, :, span]
+            remote(
+                block, block, part_send.at[side, d - 1], part_recv.at[side, d - 1], leaves[d - 1]
+            ).wait_recv()
+            piece_sum = piece_sum + got[d - 1, :, low : low + size]
+        total.append(piece_sum)
+    total = jnp.concatenate(total, 1)
     for w in range(WAVES):
         four[w, :, :OWN] = total[:, w * OWN : (w + 1) * OWN].astype(jnp.bfloat16)
     for d in FAR_WAVES:
@@ -426,7 +441,7 @@
             pltpu.VMEM((LEAF, 8, SPAN), f32),
             pltpu.VMEM((LEAF, 8, SPAN), f32),
             dma((7,)), dma((2, 4, len(CUTS))), dma((2, 4, len(CUTS))),
-            dma((LEAF - 1,)), dma((LEAF - 1,)), dma((LEAF - 1,)), dma((LEAF - 1,)),
+            dma((LEAF - 1,)), dma((LEAF - 1,)), dma((2, LEAF - 1)), dma((2, LEAF - 1)),
             dma((WAVES - 1,)), dma((WAVES - 1,)), dma((WAVES - 1,)), dma((WAVES - 1,)),
             dma((LEAF - 1,)), dma((LEAF - 1,)), dma((LEAF - 1,)), dma((LEAF - 1,)),
         ],

time: 70.1 us -> 69.9 us (level)
  no operation moved by 1% of the time
where the time goes in v9:
time: 69.9 us; the launch traced here: 69.7 us
  Pallas kernels  69.1 us (99%)
    pallas_call x1, Pallas kernels, per_device(): pl.pallas_call(whole_kernel, out_shape=(jax.ShapeDtypeStruct((GRID_ROWS,...  67 us
    pallas_call x1, Pallas kernels, per_device(): pl.pallas_call(put_kernel, out_shape=(jax.ShapeDtypeStruct(grid.shape, bf...  2.06 us

profile of v9, /device:TPU:1, one launch (start us, length us, event | category | flops | bytes accessed | tf_op | source)
XLA Modules:
  0.0 69.7 jit_solution(10290301065785505421)
XLA Ops:
  0.6 67.0 %whole.1 = (bf16[50,2,4864]{2,1,0:T(2,128)(2,1)}, f32[2,2,1280]{2,1,0:T(2,128)}) custom-call(s32[24]{0:T(128)} %map_ref.1, s32[1200]{0:T(1024)} %len_ref.1, f32[1200]{0:T(1024)} %weight_ref.1, bf16[20,2,1200]{2,1,0:T(2,128)(2,1)} %bitcast.10, bf16[2,2,1280]{2,1,0:T(2,128)(2,1)} %bitcast.11, bf16[96,256]{1,0:T(8,128)(2,1)} %constant.6.clone.spread_ref, ...), custom_call_target="tpu_custom_call" | custom-call | tf_op jit(solution)/shard_map/whole/pallas_call | solution.py:413
  67.7 2.1 %put.1 = (bf16[50,2,4864]{2,1,0:T(2,128)(2,1)}, f32[2,2,1280]{2,1,0:T(2,128)}) custom-call(bf16[50,2,4864]{2,1,0:T(2,128)(2,1)} %get-tuple-element.6.source, f32[2,2,1280]{2,1,0:T(2,128)} %get-tuple-element.7.small_source), custom_call_target="tpu_custom_call" | custom-call | tf_op jit(solution)/shard_map/put/pallas_call | solution.py:451
